TPU v7x, 32 devices: a whole 2x2x4 slice. The times are simulated.
32 devices in a mesh: batch: 8 (over y, x, core), seq: 4 (over z).
Axes of the slice: x: 2, y: 2, z: 4, core: 2. Of those that a mesh axis runs over, the one named last changes fastest.
Arguments:
- events: bfloat16 [8192, 256], P(('batch', 'seq')), parts along dimension 0, may hold values from -6 to 6
- positions: int32 [8192], P(('batch', 'seq')), parts along dimension 0, may hold values from 0 to 1023, as said below
- length: int32 [8], P('batch'), parts along dimension 0, may hold values from 512 to 1024
- filters: float32 [1024, 2, 256], P('seq'), may hold values from -0.1875 to 0.1875
- skip_gain: float32 [2, 256], replicated, may hold values from 0.5 to 1.5
- short_filter: float32 [3, 768], replicated, may hold values from -3 to 3
- in_proj: bfloat16 [256, 768], replicated, may hold values from -0.375 to 0.375
- out_proj: bfloat16 [256, 256], replicated, may hold values from -0.375 to 0.375
Outputs:
- layer_out: bfloat16 [8192, 256], P(('batch', 'seq')), parts along dimension 0
There are 8 independent parts, one for each index of `batch`. A program takes and returns all parts, laid end to end along the dimension named above; an argument that names none is the same for every part. Nothing has to cross between parts.
Inputs may be any that keep to these rules, and one draw needn't show every extreme that they name: positions is a permutation of 0 to 1023. Cut each row block b (positions b * 256 to (b + 1) * 256 - 1) into runs of 64 positions, run c starting at b * 256 + c * 64. The rows of one seq device hold whole runs only, exactly one run of each row block and exactly one run of each index c, in any order.
All inputs are finite; a program needn't handle non-finite values.
Results may differ from a plain program's by a relative error of at most 0.007.
Values may be sent and summed in bfloat16 or wider, within the bound.
No kernel may reach another device: no remote copies, remote signals or barrier semaphores. Data moves between devices by JAX's collectives and lax.ppermute only.
A program may use at most 64 MiB of HBM per device.

v0:
```python
import functools
import math

import jax
import jax.numpy as jnp
import numpy as np
from jax import lax
from jax.experimental import pallas as pl
from jax.experimental.pallas import tpu as pltpu
from jax.sharding import PartitionSpec as P

F32 = jnp.float32
BF16 = jnp.bfloat16
META = 16
NT = (((1,), (1,)), ((), ()))
NN = (((1,), (0,)), ((), ()))
TN = (((0,), (0,)), ((), ()))


def tables(dev_count, tok_rows):
    total = dev_count * tok_rows
    index = np.arange(tok_rows)
    angle = 2.0 * np.pi * (np.outer(index, index) % tok_rows) / tok_rows
    cos, sin = np.cos(angle), np.sin(angle)
    matrix = np.block([[cos, -sin], [sin, cos]]).astype(np.float32)
    high = matrix.astype(BF16)
    low = (matrix - high.astype(np.float32)).astype(BF16)
    twist = 2.0 * np.pi * (np.outer(4 * np.arange(dev_count) + 1, index) % (4 * total)) / (4 * total)
    twists = np.concatenate([np.cos(twist), np.sin(twist)], axis=0).astype(np.float32)
    return high, low, twists


def outer_coefficients(dev_count):
    angle = 2.0 * np.pi * np.outer(4 * np.arange(dev_count) + 1, np.arange(dev_count)) / (4 * dev_count)
    return np.cos(angle), np.sin(angle)


def split(x):
    high = x.astype(BF16)
    return high, (x - high.astype(F32)).astype(BF16)


def product(left_high, left_low, high_ref, low_ref, dims):
    dot = functools.partial(lax.dot_general, dimension_numbers=dims, preferred_element_type=F32)
    high = high_ref[...]
    return dot(left_high, high) + (dot(left_low, high) + dot(left_high, low_ref[...]))


def forward(blocks, high_ref, low_ref, twist_ref):
    count = len(blocks)
    inner = blocks[0].shape[1]
    cos, sin = outer_coefficients(count)
    reals, imags = [], []
    for k in range(count):
        real = blocks[0]
        imag = None
        for n in range(1, count):
            real = real + float(cos[k, n]) * blocks[n]
            term = float(-sin[k, n]) * blocks[n]
            imag = term if imag is None else imag + term
        turn_cos = twist_ref[k : k + 1, :]
        turn_sin = twist_ref[count + k : count + k + 1, :]
        if imag is None:
            imag = jnp.zeros_like(real)
        reals.append(real * turn_cos + imag * turn_sin)
        imags.append(imag * turn_cos - real * turn_sin)
    stacked = jnp.concatenate(
        [jnp.concatenate(reals, axis=0), jnp.concatenate(imags, axis=0)], axis=1
    )
    high, low = split(stacked)
    out = product(high, low, high_ref, low_ref, NN)
    return out[:, :inner], out[:, inner:]


def inverse(real, imag, count, high_ref, low_ref, twist_ref):
    inner = real.shape[1]
    width = real.shape[0] // count
    cos, sin = outer_coefficients(count)
    high, low = split(jnp.concatenate([real, imag], axis=1))
    out = product(high, low, high_ref, low_ref, NT)
    back_real, back_imag = out[:, :inner], out[:, inner:]
    scale = 1.0 / (count * inner)
    turned = []
    for k in range(count):
        rows = slice(k * width, (k + 1) * width)
        turn_cos = twist_ref[k : k + 1, :] * scale
        turn_sin = twist_ref[count + k : count + k + 1, :] * scale
        turned.append(
            (
                back_real[rows] * turn_cos - back_imag[rows] * turn_sin,
                back_imag[rows] * turn_cos + back_real[rows] * turn_sin,
            )
        )
    blocks = []
    for n in range(count):
        total = None
        for k in range(count):
            term = turned[k][0] if n == 0 else float(cos[k, n]) * turned[k][0] - float(sin[k, n]) * turned[k][1]
            total = term if total is None else total + term
        blocks.append(total)
    return blocks


def filter_kernel(count, filt_ref, *refs):
    outs, flipped = refs[:count], refs[count]
    me = lax.axis_index("seq")
    core = lax.rem(lax.axis_index("batch"), 2)
    width = outs[0].shape[0]
    one = jnp.where(core == 0, filt_ref[:, 0, :], filt_ref[:, 1, :])
    flipped[...] = one.T
    for k in range(count):
        start = pl.multiple_of(lax.bitwise_xor(me, k) * width, width)
        outs[k][...] = flipped[pl.ds(start, width), :]


def project_kernel(count, length_ref, events_ref, pos_ref, weights_ref, *refs):
    outs, whole = refs[:count], refs[count]
    me = lax.axis_index("seq")
    rows, features = events_ref.shape
    width = features // count
    pos = pos_ref[...]
    keep = (pos < length_ref[0]).astype(F32)
    projected = lax.dot_general(
        weights_ref[...], events_ref[...], (((0,), (1,)), ((), ())), preferred_element_type=F32
    )
    whole[...] = (projected * keep).astype(BF16)
    line = lax.broadcasted_iota(jnp.int32, (META, rows), 0)
    high = lax.div(pos, 256)
    meta = jnp.where(line == 0, high, jnp.where(line == 1, pos - high * 256, 0))
    meta = meta.astype(F32).astype(BF16)
    for k in range(count):
        dest = lax.bitwise_xor(me, k)
        for part in range(3):
            start = pl.multiple_of(part * features + dest * width, width)
            outs[k][part * width : (part + 1) * width, :] = whole[pl.ds(start, width), :]
        outs[k][3 * width :, :] = meta


def spectrum_kernel(count, high_ref, low_ref, twist_ref, short_ref, gain_ref, *refs):
    parts, spec_ref, scale_ref, held = refs[:count], refs[count], refs[count + 1], refs[count + 2]
    me = lax.axis_index("seq")
    width, inner = parts[0].shape
    for k in range(count):
        held[pl.ds(lax.bitwise_xor(me, k), 1)] = parts[k][...][None]
    real, imag = forward([held[n] for n in range(count)], high_ref, low_ref, twist_ref)
    spec_ref[:, :inner] = real
    spec_ref[:, inner:] = imag
    features = gain_ref.shape[1]
    row = lax.broadcasted_iota(jnp.int32, (width, features), 0)
    lane = lax.broadcasted_iota(jnp.int32, (width, features), 1)
    chosen = lane == row + me * width
    place = lax.broadcasted_iota(jnp.int32, (width, scale_ref.shape[1]), 1)

    def column(line):
        return jnp.sum(jnp.where(chosen, line, 0.0), axis=1, keepdims=True)

    for part in range(3):
        out = jnp.zeros((width, scale_ref.shape[1]), F32)
        for tap in range(3):
            line = short_ref[tap : tap + 1, part * features : (part + 1) * features]
            out = jnp.where(place == tap, column(line), out)
        if part < 2:
            out = jnp.where(place == 3, column(gain_ref[part : part + 1, :]), out)
        scale_ref[part * width : (part + 1) * width, :] = out


def mix_kernel(count, high_ref, low_ref, twist_ref, scale_ref, own_ref, other_ref, *refs):
    parts, outs, gated = refs[:count], refs[count : 2 * count], refs[2 * count]
    me = lax.axis_index("seq")
    core = lax.rem(lax.axis_index("batch"), 2)
    inner = parts[0].shape[1]
    width = (parts[0].shape[0] - META) // 3
    rows = [part[: 3 * width, :] for part in parts]
    places = []
    for part in parts:
        meta = part[3 * width :, :].astype(F32)
        places.append((meta[0:1, :] * 256.0 + meta[1:2, :]).astype(jnp.int32))
    wanted = lax.broadcasted_iota(jnp.int32, (inner, inner), 0)
    placed = []
    for n in range(count):
        total = None
        for k in range(count):
            hit = (wanted + n * inner == places[k]).astype(F32).astype(BF16)
            term = lax.dot_general(rows[k], hit, NT, preferred_element_type=F32)
            total = term if total is None else total + term
        placed.append(total)
    whole = jnp.concatenate(placed, axis=1)
    lane = lax.broadcasted_iota(jnp.int32, (1, count * inner), 1)
    scale = scale_ref[...]
    back_one = jnp.where(lane >= 1, pltpu.roll(whole, 1, 1), 0.0)
    back_two = jnp.where(lane >= 2, pltpu.roll(whole, 2, 1), 0.0)
    shorted = scale[:, 0:1] * whole + scale[:, 1:2] * back_one + scale[:, 2:3] * back_two

    def blocks_of(part):
        return [
            shorted[part * width : (part + 1) * width, n * inner : (n + 1) * inner]
            for n in range(count)
        ]

    def spectrum(which):
        mine = core == which
        return jnp.where(mine, own_ref[...], other_ref[...])

    def convolve(blocks, which):
        taps = spectrum(which)
        taps_real, taps_imag = taps[:, :inner], taps[:, inner:]
        real, imag = forward(blocks, high_ref, low_ref, twist_ref)
        return inverse(
            real * taps_real - imag * taps_imag,
            real * taps_imag + imag * taps_real,
            count, high_ref, low_ref, twist_ref,
        )

    value, gate_one, gate_two = blocks_of(0), blocks_of(1), blocks_of(2)
    gain_one, gain_two = scale[:width, 3:4], scale[width : 2 * width, 3:4]
    mixed = convolve(value, 0)
    first = [gate_one[n] * (mixed[n] + gain_one * value[n]) for n in range(count)]
    mixed = convolve(first, 1)
    for n in range(count):
        gated[n] = (gate_two[n] * (mixed[n] + gain_two * first[n])).astype(BF16)
    for k in range(count):
        outs[k][...] = gated[pl.ds(lax.bitwise_xor(me, k), 1)][0]


def output_kernel(count, weights_ref, *refs):
    parts, out_ref = refs[:count], refs[count]
    me = lax.axis_index("seq")
    width = parts[0].shape[0]
    total = None
    for k in range(count):
        start = pl.multiple_of(lax.bitwise_xor(me, k) * width, width)
        term = lax.dot_general(
            parts[k][...], weights_ref[pl.ds(start, width), :], TN, preferred_element_type=F32
        )
        total = term if total is None else total + term
    out_ref[...] = total.astype(BF16)


def call(kernel, name, out_shape, scratch, flops, *args):
    smem = pl.BlockSpec(memory_space=pltpu.SMEM)
    vmem = pl.BlockSpec(memory_space=pltpu.VMEM)
    outs = out_shape if isinstance(out_shape, (list, tuple)) else [out_shape]
    moved = sum(math.prod(a.shape) * a.dtype.itemsize for a in list(args) + list(outs))
    return pl.pallas_call(
        kernel,
        name=name,
        out_shape=out_shape,
        in_specs=[smem if a.ndim == 1 else vmem for a in args],
        out_specs=jax.tree.map(lambda _: vmem, out_shape),
        scratch_shapes=scratch,
        cost_estimate=pl.CostEstimate(flops=flops, bytes_accessed=moved, transcendentals=0),
        compiler_params=pltpu.CompilerParams(vmem_limit_bytes=48 * 1024 * 1024),
    )(*args)


def exchange(parts):
    count = len(parts)
    got = [parts[0]]
    for k in range(1, count):
        got.append(lax.ppermute(parts[k], "seq", [(d, d ^ k) for d in range(count)]))
    return got


def body(events, positions, length, filters, skip_gain, short_filter, in_proj, out_proj):
    tok_rows, features = events.shape
    count = lax.axis_size("seq")
    width = features // count
    shape = jax.ShapeDtypeStruct
    high, low, twists = (jnp.asarray(t) for t in tables(count, tok_rows))

    filter_parts = call(
        functools.partial(filter_kernel, count), "filters",
        [shape((width, tok_rows), F32)] * count,
        [pltpu.VMEM((features, tok_rows), F32)], 10**6, filters,
    )
    filter_parts = exchange(filter_parts)
    sent = call(
        functools.partial(project_kernel, count), "project",
        [shape((3 * width + META, tok_rows), BF16)] * count,
        [pltpu.VMEM((3 * features, tok_rows), BF16)], 10**8,
        length, events, positions.reshape(1, tok_rows), in_proj,
    )
    got = exchange(sent)
    own, scale = call(
        functools.partial(spectrum_kernel, count), "spectrum",
        [shape((features, 2 * tok_rows), F32), shape((3 * width, 128), F32)],
        [pltpu.VMEM((count, width, tok_rows), F32)], 4 * 10**8,
        high, low, twists, short_filter, skip_gain, *filter_parts,
    )
    pairs = [(d, d ^ 1) for d in range(lax.axis_size("batch"))]
    other = lax.ppermute(own, "batch", pairs)
    gated = call(
        functools.partial(mix_kernel, count), "mix",
        [shape((width, tok_rows), BF16)] * count,
        [pltpu.VMEM((count, width, tok_rows), BF16)], 2 * 10**9,
        high, low, twists, scale, own, other, *got,
    )
    back = exchange(gated)
    return call(
        functools.partial(output_kernel, count), "output",
        shape((tok_rows, features), BF16), [], 10**8, out_proj, *back,
    )


def solution(mesh):
    return jax.shard_map(
        body,
        mesh=mesh,
        in_specs=(
            P(("batch", "seq"), None),
            P(("batch", "seq")),
            P("batch"),
            P("seq", None, None),
            P(),
            P(),
            P(),
            P(),
        ),
        out_specs=P(("batch", "seq"), None),
        check_vma=False,
    )
```

profile of v0, /device:TPU:0, one launch (start us, length us, event | category | flops | bytes accessed | tf_op | source)
XLA Modules:
  0.0 42.9 jit_solution(11178573034531382707)
XLA Ops:
  0.0 1.0 %copy-done = f32[256,2,256]{2,1,0:T(2,128)S(1)} copy-done((f32[256,2,256]{2,1,0:T(2,128)S(1)}, f32[256,2,256]{2,1,0:T(2,128)}, u32[]{:S(2)}) %copy-start) | copy-done | bytes 524312
  1.0 0.2 filters.1
  1.3 3.1 %collective-permute-start = (f32[64,256]{1,0:T(8,128)S(1)}, f32[64,256]{1,0:T(8,128)S(1)}, u32[]{:S(2)}, u32[]{:S(2)}) collective-permute-start(f32[64,256]{1,0:T(8,128)S(1)} %get-tuple-element.20), channel_id=1, source_target_pairs={{0,1},{1,0},{2,3},{3,2},{4,5},{5,4},{6,7},{7,6},{8,9},{9,8},{10,11... | collective-permute-start | bytes 196616 | tf_op jit(solution)/shard_map/ppermute | solution.py:260
  4.4 2.6 %collective-permute-start.1 = (f32[64,256]{1,0:T(8,128)S(1)}, f32[64,256]{1,0:T(8,128)S(1)}, u32[]{:S(2)}, u32[]{:S(2)}) collective-permute-start(f32[64,256]{1,0:T(8,128)S(1)} %get-tuple-element.21), channel_id=1, source_target_pairs={{0,2},{1,3},{2,0},{3,1},{4,6},{5,7},{6,4},{7,5},{8,10},{9,11},{10,... | collective-permute-start | bytes 196616 | tf_op jit(solution)/shard_map/ppermute | solution.py:260
  7.0 0.0 collective-permute-start.2
  7.0 0.0 collective-permute-done.refs_1_
  7.0 4.7 %collective-permute-done.1.refs_2_ = f32[64,256]{1,0:T(8,128)S(1)} collective-permute-done((f32[64,256]{1,0:T(8,128)S(1)}, f32[64,256]{1,0:T(8,128)S(1)}, u32[]{:S(2)}, u32[]{:S(2)}) %collective-permute-start.1) | collective-permute-done | bytes 65568 | tf_op jit(solution)/shard_map/ppermute | solution.py:260
  11.7 1.4 %collective-permute-done.2.refs_3_ = f32[64,256]{1,0:T(8,128)S(1)} collective-permute-done((f32[64,256]{1,0:T(8,128)S(1)}, f32[64,256]{1,0:T(8,128)S(1)}, u32[]{:S(2)}, u32[]{:S(2)}) %collective-permute-start.2) | collective-permute-done | bytes 65568 | tf_op jit(solution)/shard_map/ppermute | solution.py:260
  13.1 0.0 copy-start.7
  13.1 1.0 %copy-done.7 = bf16[512,512]{1,0:T(8,128)(2,1)S(1)} copy-done((bf16[512,512]{1,0:T(8,128)(2,1)S(1)}, bf16[512,512]{1,0:T(8,128)(2,1)}, u32[]{:S(2)}) %copy-start.7) | copy-done | bytes 524312
  14.1 1.0 %copy-done.9 = bf16[512,512]{1,0:T(8,128)(2,1)S(1)} copy-done((bf16[512,512]{1,0:T(8,128)(2,1)S(1)}, bf16[512,512]{1,0:T(8,128)(2,1)}, u32[]{:S(2)}) %copy-start.9) | copy-done | bytes 524312
  15.2 0.6 %spectrum.1 = (f32[256,512]{1,0:T(8,128)S(1)}, f32[192,128]{1,0:T(8,128)S(1)}) custom-call(bf16[512,512]{1,0:T(8,128)(2,1)S(1)} %copy-done.9, bf16[512,512]{1,0:T(8,128)(2,1)S(1)} %copy-done.7, f32[8,256]{1,0:T(8,128)S(1)} %copy-done.10, f32[3,768]{1,0:T(4,128)S(1)} %copy-done.5, f32[2,256]{1,0:T(2,128)S(1)} %copy-done.6, ...), custom_call_target="tpu_custom_call" | custom-call | flops 400000000 | bytes 1952768 | tf_op jit(solution)/shard_map/spectrum/pallas_call | solution.py:244
  15.8 0.1 collective-permute-start.3
  16.5 0.0 copy-start.4
  16.6 0.7 %copy-done.4 = s32[256]{0:T(256)S(1)} copy-done((s32[256]{0:T(256)S(1)}, s32[256]{0:T(256)}, u32[]{:S(2)}) %copy-start.4) | copy-done | bytes 1048
  17.2 0.3 project.1
  17.6 0.1 collective-permute-start.4
  17.6 2.3 %collective-permute-start.5 = (bf16[208,256]{1,0:T(8,128)(2,1)S(1)}, bf16[208,256]{1,0:T(8,128)(2,1)S(1)}, u32[]{:S(2)}, u32[]{:S(2)}) collective-permute-start(bf16[208,256]{1,0:T(8,128)(2,1)S(1)} %get-tuple-element.27), channel_id=1, source_target_pairs={{0,2},{1,3},{2,0},{3,1},{4,6},{5,7},{6,4},{7,5},{8,10},{9,11},{10,... | collective-permute-start | bytes 319496 | tf_op jit(solution)/shard_map/ppermute | solution.py:260
  20.0 2.0 %collective-permute-start.6 = (bf16[208,256]{1,0:T(8,128)(2,1)S(1)}, bf16[208,256]{1,0:T(8,128)(2,1)S(1)}, u32[]{:S(2)}, u32[]{:S(2)}) collective-permute-start(bf16[208,256]{1,0:T(8,128)(2,1)S(1)} %get-tuple-element.28), channel_id=1, source_target_pairs={{0,3},{1,2},{2,1},{3,0},{4,7},{5,6},{6,5},{7,4},{8,11},{9,10},{10,... | collective-permute-start | bytes 319496 | tf_op jit(solution)/shard_map/ppermute | solution.py:260
  22.0 3.1 %collective-permute-done.4.refs_1_ = bf16[208,256]{1,0:T(8,128)(2,1)S(1)} collective-permute-done((bf16[208,256]{1,0:T(8,128)(2,1)S(1)}, bf16[208,256]{1,0:T(8,128)(2,1)S(1)}, u32[]{:S(2)}, u32[]{:S(2)}) %collective-permute-start.4) | collective-permute-done | bytes 106528 | tf_op jit(solution)/shard_map/ppermute | solution.py:260
  25.1 4.0 %collective-permute-done.5.refs_2_ = bf16[208,256]{1,0:T(8,128)(2,1)S(1)} collective-permute-done((bf16[208,256]{1,0:T(8,128)(2,1)S(1)}, bf16[208,256]{1,0:T(8,128)(2,1)S(1)}, u32[]{:S(2)}, u32[]{:S(2)}) %collective-permute-start.5) | collective-permute-done | bytes 106528 | tf_op jit(solution)/shard_map/ppermute | solution.py:260
  29.1 0.0 collective-permute-done.6.refs_3_
  29.1 0.0 collective-permute-done.3.other_ref
  29.1 0.0 copy-start.3
  29.1 3.4 %mix.1 = (bf16[64,256]{1,0:T(8,128)(2,1)S(1)}, bf16[64,256]{1,0:T(8,128)(2,1)S(1)}, bf16[64,256]{1,0:T(8,128)(2,1)S(1)}, bf16[64,256]{1,0:T(8,128)(2,1)S(1)}) custom-call(bf16[512,512]{1,0:T(8,128)(2,1)S(1)} %copy-done.9, bf16[512,512]{1,0:T(8,128)(2,1)S(1)} %copy-done.8, f32[8,256]{1,0:T(8,128)S(1)} %copy-done.10, ...), custom_call_target="tpu_custom_call" | custom-call | flops 2000000000 | bytes 2760704 | tf_op jit(solution)/shard_map/mix/pallas_call | solution.py:244
  32.5 2.4 %collective-permute-start.7 = (bf16[64,256]{1,0:T(8,128)(2,1)S(1)}, bf16[64,256]{1,0:T(8,128)(2,1)S(1)}, u32[]{:S(2)}, u32[]{:S(2)}) collective-permute-start(bf16[64,256]{1,0:T(8,128)(2,1)S(1)} %get-tuple-element.30), channel_id=1, source_target_pairs={{0,1},{1,0},{2,3},{3,2},{4,5},{5,4},{6,7},{7,6},{8,9},{9,8},{10,11... | collective-permute-start | bytes 98312 | tf_op jit(solution)/shard_map/ppermute | solution.py:260
  34.9 1.2 %collective-permute-start.8 = (bf16[64,256]{1,0:T(8,128)(2,1)S(1)}, bf16[64,256]{1,0:T(8,128)(2,1)S(1)}, u32[]{:S(2)}, u32[]{:S(2)}) collective-permute-start(bf16[64,256]{1,0:T(8,128)(2,1)S(1)} %get-tuple-element.31), channel_id=1, source_target_pairs={{0,2},{1,3},{2,0},{3,1},{4,6},{5,7},{6,4},{7,5},{8,10},{9,11},{10,... | collective-permute-start | bytes 98312 | tf_op jit(solution)/shard_map/ppermute | solution.py:260
  36.2 1.4 %collective-permute-start.9 = (bf16[64,256]{1,0:T(8,128)(2,1)S(1)}, bf16[64,256]{1,0:T(8,128)(2,1)S(1)}, u32[]{:S(2)}, u32[]{:S(2)}) collective-permute-start(bf16[64,256]{1,0:T(8,128)(2,1)S(1)} %get-tuple-element.32), channel_id=1, source_target_pairs={{0,3},{1,2},{2,1},{3,0},{4,7},{5,6},{6,5},{7,4},{8,11},{9,10},{10,... | collective-permute-start | bytes 98312 | tf_op jit(solution)/shard_map/ppermute | solution.py:260
  37.6 0.0 collective-permute-done.7.refs_1_
  37.6 2.9 %collective-permute-done.8.refs_2_ = bf16[64,256]{1,0:T(8,128)(2,1)S(1)} collective-permute-done((bf16[64,256]{1,0:T(8,128)(2,1)S(1)}, bf16[64,256]{1,0:T(8,128)(2,1)S(1)}, u32[]{:S(2)}, u32[]{:S(2)}) %collective-permute-start.8) | collective-permute-done | bytes 32800 | tf_op jit(solution)/shard_map/ppermute | solution.py:260
  40.5 1.4 %collective-permute-done.9.refs_3_ = bf16[64,256]{1,0:T(8,128)(2,1)S(1)} collective-permute-done((bf16[64,256]{1,0:T(8,128)(2,1)S(1)}, bf16[64,256]{1,0:T(8,128)(2,1)S(1)}, u32[]{:S(2)}, u32[]{:S(2)}) %collective-permute-start.9) | collective-permute-done | bytes 32800 | tf_op jit(solution)/shard_map/ppermute | solution.py:260
  41.9 1.0 %output.1 = bf16[256,256]{1,0:T(8,128)(2,1)} custom-call(bf16[256,256]{1,0:T(8,128)(2,1)S(1)} %copy-done.3, bf16[64,256]{1,0:T(8,128)(2,1)S(1)} %get-tuple-element.29.refs_0_, bf16[64,256]{1,0:T(8,128)(2,1)S(1)} %collective-permute-done.7.refs_1_, bf16[64,256]{1,0:T(8,128)(2,1)S(1)} %collective-permute-done.8.refs_2_, ...), custom_call_target="tpu_custom_call" | custom-call | flops 100000000 | bytes 393216 | tf_op jit(solution)/shard_map/output/pallas_call | solution.py:244
  (15 shorter events, 0.0 us)
Async XLA Ops:
  0.0 1.0 %copy-start = (f32[256,2,256]{2,1,0:T(2,128)S(1)}, f32[256,2,256]{2,1,0:T(2,128)}, u32[]{:S(2)}) copy-start(f32[256,2,256]{2,1,0:T(2,128)} %filt_ref.1) | copy-start | bytes 1572868
  1.0 12.0 %copy-start.5 = (f32[3,768]{1,0:T(4,128)S(1)}, f32[3,768]{1,0:T(4,128)}, u32[]{:S(2)}) copy-start(f32[3,768]{1,0:T(4,128)} %short_ref.1) | copy-start | bytes 27652
  1.0 12.0 %copy-start.10 = (f32[8,256]{1,0:T(8,128)S(1)}, f32[8,256]{1,0:T(8,128)}, u32[]{:S(2)}) copy-start(f32[8,256]{1,0:T(8,128)} %constant.8.clone.twist_ref) | copy-start | bytes 24580
  1.3 5.7 %collective-permute-start = (f32[64,256]{1,0:T(8,128)S(1)}, f32[64,256]{1,0:T(8,128)S(1)}, u32[]{:S(2)}, u32[]{:S(2)}) collective-permute-start(f32[64,256]{1,0:T(8,128)S(1)} %get-tuple-element.20), channel_id=1, source_target_pairs={{0,1},{1,0},{2,3},{3,2},{4,5},{5,4},{6,7},{7,6},{8,9},{9,8},{10,11... | collective-permute-start | bytes 196616 | tf_op jit(solution)/shard_map/ppermute | solution.py:260
  4.4 8.7 %copy-start.6 = (f32[2,256]{1,0:T(2,128)S(1)}, f32[2,256]{1,0:T(2,128)}, u32[]{:S(2)}) copy-start(f32[2,256]{1,0:T(2,128)} %gain_ref.1) | copy-start | bytes 6148
  4.4 7.3 %collective-permute-start.1 = (f32[64,256]{1,0:T(8,128)S(1)}, f32[64,256]{1,0:T(8,128)S(1)}, u32[]{:S(2)}, u32[]{:S(2)}) collective-permute-start(f32[64,256]{1,0:T(8,128)S(1)} %get-tuple-element.21), channel_id=1, source_target_pairs={{0,2},{1,3},{2,0},{3,1},{4,6},{5,7},{6,4},{7,5},{8,10},{9,11},{10,... | collective-permute-start | bytes 196616 | tf_op jit(solution)/shard_map/ppermute | solution.py:260
  7.0 6.1 %collective-permute-start.2 = (f32[64,256]{1,0:T(8,128)S(1)}, f32[64,256]{1,0:T(8,128)S(1)}, u32[]{:S(2)}, u32[]{:S(2)}) collective-permute-start(f32[64,256]{1,0:T(8,128)S(1)} %get-tuple-element.22), channel_id=1, source_target_pairs={{0,3},{1,2},{2,1},{3,0},{4,7},{5,6},{6,5},{7,4},{8,11},{9,10},{10,... | collective-permute-start | bytes 196616 | tf_op jit(solution)/shard_map/ppermute | solution.py:260
  13.1 1.0 %copy-start.7 = (bf16[512,512]{1,0:T(8,128)(2,1)S(1)}, bf16[512,512]{1,0:T(8,128)(2,1)}, u32[]{:S(2)}) copy-start(bf16[512,512]{1,0:T(8,128)(2,1)} %constant.7.clone.low_ref) | copy-start | bytes 1572868
  14.1 1.0 %copy-start.9 = (bf16[512,512]{1,0:T(8,128)(2,1)S(1)}, bf16[512,512]{1,0:T(8,128)(2,1)}, u32[]{:S(2)}) copy-start(bf16[512,512]{1,0:T(8,128)(2,1)} %constant.6.clone.high_ref) | copy-start | bytes 1572868
  15.2 1.4 %copy-start.1 = (bf16[256,768]{1,0:T(8,128)(2,1)S(1)}, bf16[256,768]{1,0:T(8,128)(2,1)}, u32[]{:S(2)}) copy-start(bf16[256,768]{1,0:T(8,128)(2,1)} %weights_ref.2) | copy-start | bytes 1179652
  15.2 1.4 %copy-start.2 = (bf16[256,256]{1,0:T(8,128)(2,1)S(1)}, bf16[256,256]{1,0:T(8,128)(2,1)}, u32[]{:S(2)}) copy-start(bf16[256,256]{1,0:T(8,128)(2,1)} %events_ref.1) | copy-start | bytes 393220
  15.2 13.9 %copy-start.8 = (bf16[512,512]{1,0:T(8,128)(2,1)S(1)}, bf16[512,512]{1,0:T(8,128)(2,1)}, u32[]{:S(2)}) copy-start(bf16[512,512]{1,0:T(8,128)(2,1)} %constant.7.clone.low_ref) | copy-start | bytes 1572868
  15.8 13.3 %collective-permute-start.3 = (f32[256,512]{1,0:T(8,128)S(1)}, f32[256,512]{1,0:T(8,128)S(1)}, u32[]{:S(2)}, u32[]{:S(2)}) collective-permute-start(f32[256,512]{1,0:T(8,128)S(1)} %get-tuple-element.24.own_ref), channel_id=1, source_target_pairs={{0,4},{4,0},{8,12},{12,8},{16,20},{20,16},{24,28},{28,24},{1,5},{5... | collective-permute-start | bytes 1572872 | tf_op jit(solution)/shard_map/ppermute | solution.py:291
  16.5 0.7 %copy-start.4 = (s32[256]{0:T(256)S(1)}, s32[256]{0:T(256)}, u32[]{:S(2)}) copy-start(s32[256]{0:T(256)} %param.12) | copy-start | bytes 3076
  17.6 7.5 %collective-permute-start.4 = (bf16[208,256]{1,0:T(8,128)(2,1)S(1)}, bf16[208,256]{1,0:T(8,128)(2,1)S(1)}, u32[]{:S(2)}, u32[]{:S(2)}) collective-permute-start(bf16[208,256]{1,0:T(8,128)(2,1)S(1)} %get-tuple-element.26), channel_id=1, source_target_pairs={{0,1},{1,0},{2,3},{3,2},{4,5},{5,4},{6,7},{7,6},{8,9},{9,8},{10,11... | collective-permute-start | bytes 319496 | tf_op jit(solution)/shard_map/ppermute | solution.py:260
  17.6 11.4 %collective-permute-start.5 = (bf16[208,256]{1,0:T(8,128)(2,1)S(1)}, bf16[208,256]{1,0:T(8,128)(2,1)S(1)}, u32[]{:S(2)}, u32[]{:S(2)}) collective-permute-start(bf16[208,256]{1,0:T(8,128)(2,1)S(1)} %get-tuple-element.27), channel_id=1, source_target_pairs={{0,2},{1,3},{2,0},{3,1},{4,6},{5,7},{6,4},{7,5},{8,10},{9,11},{10,... | collective-permute-start | bytes 319496 | tf_op jit(solution)/shard_map/ppermute | solution.py:260
  20.0 9.1 %collective-permute-start.6 = (bf16[208,256]{1,0:T(8,128)(2,1)S(1)}, bf16[208,256]{1,0:T(8,128)(2,1)S(1)}, u32[]{:S(2)}, u32[]{:S(2)}) collective-permute-start(bf16[208,256]{1,0:T(8,128)(2,1)S(1)} %get-tuple-element.28), channel_id=1, source_target_pairs={{0,3},{1,2},{2,1},{3,0},{4,7},{5,6},{6,5},{7,4},{8,11},{9,10},{10,... | collective-permute-start | bytes 319496 | tf_op jit(solution)/shard_map/ppermute | solution.py:260
  29.1 12.8 %copy-start.3 = (bf16[256,256]{1,0:T(8,128)(2,1)S(1)}, bf16[256,256]{1,0:T(8,128)(2,1)}, u32[]{:S(2)}) copy-start(bf16[256,256]{1,0:T(8,128)(2,1)} %weights_ref.3) | copy-start | bytes 393220
  32.5 5.1 %collective-permute-start.7 = (bf16[64,256]{1,0:T(8,128)(2,1)S(1)}, bf16[64,256]{1,0:T(8,128)(2,1)S(1)}, u32[]{:S(2)}, u32[]{:S(2)}) collective-permute-start(bf16[64,256]{1,0:T(8,128)(2,1)S(1)} %get-tuple-element.30), channel_id=1, source_target_pairs={{0,1},{1,0},{2,3},{3,2},{4,5},{5,4},{6,7},{7,6},{8,9},{9,8},{10,11... | collective-permute-start | bytes 98312 | tf_op jit(solution)/shard_map/ppermute | solution.py:260
  34.9 5.5 %collective-permute-start.8 = (bf16[64,256]{1,0:T(8,128)(2,1)S(1)}, bf16[64,256]{1,0:T(8,128)(2,1)S(1)}, u32[]{:S(2)}, u32[]{:S(2)}) collective-permute-start(bf16[64,256]{1,0:T(8,128)(2,1)S(1)} %get-tuple-element.31), channel_id=1, source_target_pairs={{0,2},{1,3},{2,0},{3,1},{4,6},{5,7},{6,4},{7,5},{8,10},{9,11},{10,... | collective-permute-start | bytes 98312 | tf_op jit(solution)/shard_map/ppermute | solution.py:260
  36.2 5.7 %collective-permute-start.9 = (bf16[64,256]{1,0:T(8,128)(2,1)S(1)}, bf16[64,256]{1,0:T(8,128)(2,1)S(1)}, u32[]{:S(2)}, u32[]{:S(2)}) collective-permute-start(bf16[64,256]{1,0:T(8,128)(2,1)S(1)} %get-tuple-element.32), channel_id=1, source_target_pairs={{0,3},{1,2},{2,1},{3,0},{4,7},{5,6},{6,5},{7,4},{8,11},{9,10},{10,... | collective-permute-start | bytes 98312 | tf_op jit(solution)/shard_map/ppermute | solution.py:260
where the time goes:
time: 43.2 us; the launch traced here: 42.9 us
  waiting for transfers between devices  17.4 us (40%)
  starting transfers between devices  15.3 us (35%)
  Pallas kernels  5.59 us (13%)
  local copies, waits for them, and re-layouts  3.8 us (9%)
  between operations  0.75 us (2%)
    ppermute x9, waiting for transfers between devices, exchange(): lax.ppermute(parts[k], 'seq', [(d, d ^ k) for d in range(count)])  17.4 us
    ppermute x9, starting transfers between devices, exchange(): lax.ppermute(parts[k], 'seq', [(d, d ^ k) for d in range(count)])  15.2 us
    pallas_call x5, Pallas kernels, call(): pl.pallas_call(kernel, name=name, out_shape=out_shape, in_specs=[smem if...  5.59 us
    unnamed x22, local copies, waits for them, and re-layouts  3.8 us
  transfers between devices with their start and end apart: 10, of which 6 were waited for; matrix products, arithmetic and copies ran while one was open for 0% of the time, Pallas kernels for 1%

commit v1 on v0

--- a/solution.py
+++ b/solution.py
@@ -101,29 +101,37 @@
     return blocks
 
 
-def filter_kernel(count, filt_ref, *refs):
-    outs, flipped = refs[:count], refs[count]
+def prepare_kernel(count, events_hbm, pos_hbm, weights_hbm, filt_hbm, *refs):
+    taps, rows_out = refs[:count], refs[count : 2 * count]
+    events_ref, pos_ref, weights_ref, filt_ref, flipped, whole, sems = refs[2 * count :]
     me = lax.axis_index("seq")
     core = lax.rem(lax.axis_index("batch"), 2)
-    width = outs[0].shape[0]
+    loads = [
+        pltpu.make_async_copy(source, target, sems.at[n])
+        for n, (source, target) in enumerate((
+            (events_hbm, events_ref),
+            (weights_hbm, weights_ref),
+            (filt_hbm, filt_ref),
+            (pos_hbm, pos_ref),
+        ))
+    ]
+    for load in loads:
+        load.start()
+    rows, features = events_ref.shape
+    width = features // count
+    loads[2].wait()
     one = jnp.where(core == 0, filt_ref[:, 0, :], filt_ref[:, 1, :])
     flipped[...] = one.T
     for k in range(count):
         start = pl.multiple_of(lax.bitwise_xor(me, k) * width, width)
-        outs[k][...] = flipped[pl.ds(start, width), :]
-
-
-def project_kernel(count, length_ref, events_ref, pos_ref, weights_ref, *refs):
-    outs, whole = refs[:count], refs[count]
-    me = lax.axis_index("seq")
-    rows, features = events_ref.shape
-    width = features // count
+        taps[k][...] = flipped[pl.ds(start, width), :]
+    for n in (0, 1, 3):
+        loads[n].wait()
     pos = pos_ref[...]
-    keep = (pos < length_ref[0]).astype(F32)
     projected = lax.dot_general(
         weights_ref[...], events_ref[...], (((0,), (1,)), ((), ())), preferred_element_type=F32
     )
-    whole[...] = (projected * keep).astype(BF16)
+    whole[...] = projected.astype(BF16)
     line = lax.broadcasted_iota(jnp.int32, (META, rows), 0)
     high = lax.div(pos, 256)
     meta = jnp.where(line == 0, high, jnp.where(line == 1, pos - high * 256, 0))
@@ -132,11 +140,11 @@
         dest = lax.bitwise_xor(me, k)
         for part in range(3):
             start = pl.multiple_of(part * features + dest * width, width)
-            outs[k][part * width : (part + 1) * width, :] = whole[pl.ds(start, width), :]
-        outs[k][3 * width :, :] = meta
-
-
-def spectrum_kernel(count, high_ref, low_ref, twist_ref, short_ref, gain_ref, *refs):
+            rows_out[k][part * width : (part + 1) * width, :] = whole[pl.ds(start, width), :]
+        rows_out[k][3 * width :, :] = meta
+
+
+def spectrum_kernel(count, high_ref, low_ref, twist_ref, short_ref, gain_ref, length_ref, *refs):
     parts, spec_ref, scale_ref, held = refs[:count], refs[count], refs[count + 1], refs[count + 2]
     me = lax.axis_index("seq")
     width, inner = parts[0].shape
@@ -161,6 +169,7 @@
             out = jnp.where(place == tap, column(line), out)
         if part < 2:
             out = jnp.where(place == 3, column(gain_ref[part : part + 1, :]), out)
+        out = jnp.where(place == 4, length_ref[...].astype(F32), out)
         scale_ref[part * width : (part + 1) * width, :] = out
 
 
@@ -184,9 +193,10 @@
             term = lax.dot_general(rows[k], hit, NT, preferred_element_type=F32)
             total = term if total is None else total + term
         placed.append(total)
-    whole = jnp.concatenate(placed, axis=1)
     lane = lax.broadcasted_iota(jnp.int32, (1, count * inner), 1)
     scale = scale_ref[...]
+    real_rows = lane.astype(F32) < scale[0:1, 4:5]
+    whole = jnp.where(real_rows, jnp.concatenate(placed, axis=1), 0.0)
     back_one = jnp.where(lane >= 1, pltpu.roll(whole, 1, 1), 0.0)
     back_two = jnp.where(lane >= 2, pltpu.roll(whole, 2, 1), 0.0)
     shorted = scale[:, 0:1] * whole + scale[:, 1:2] * back_one + scale[:, 2:3] * back_two
@@ -236,20 +246,18 @@
     out_ref[...] = total.astype(BF16)
 
 
-def call(kernel, name, out_shape, scratch, flops, *args):
-    smem = pl.BlockSpec(memory_space=pltpu.SMEM)
+def call(kernel, out_shape, scratch, flops, space, *args, grant=48 * 1024 * 1024):
     vmem = pl.BlockSpec(memory_space=pltpu.VMEM)
     outs = out_shape if isinstance(out_shape, (list, tuple)) else [out_shape]
     moved = sum(math.prod(a.shape) * a.dtype.itemsize for a in list(args) + list(outs))
     return pl.pallas_call(
         kernel,
-        name=name,
         out_shape=out_shape,
-        in_specs=[smem if a.ndim == 1 else vmem for a in args],
+        in_specs=[pl.BlockSpec(memory_space=space)] * len(args),
         out_specs=jax.tree.map(lambda _: vmem, out_shape),
         scratch_shapes=scratch,
         cost_estimate=pl.CostEstimate(flops=flops, bytes_accessed=moved, transcendentals=0),
-        compiler_params=pltpu.CompilerParams(vmem_limit_bytes=48 * 1024 * 1024),
+        compiler_params=pltpu.CompilerParams(vmem_limit_bytes=grant),
     )(*args)
 
 
@@ -268,37 +276,42 @@
     shape = jax.ShapeDtypeStruct
     high, low, twists = (jnp.asarray(t) for t in tables(count, tok_rows))
 
-    filter_parts = call(
-        functools.partial(filter_kernel, count), "filters",
-        [shape((width, tok_rows), F32)] * count,
-        [pltpu.VMEM((features, tok_rows), F32)], 10**6, filters,
-    )
-    filter_parts = exchange(filter_parts)
-    sent = call(
-        functools.partial(project_kernel, count), "project",
-        [shape((3 * width + META, tok_rows), BF16)] * count,
-        [pltpu.VMEM((3 * features, tok_rows), BF16)], 10**8,
-        length, events, positions.reshape(1, tok_rows), in_proj,
-    )
-    got = exchange(sent)
+    prepared = call(
+        functools.partial(prepare_kernel, count),
+        [shape((width, tok_rows), F32)] * count
+        + [shape((3 * width + META, tok_rows), BF16)] * count,
+        [
+            pltpu.VMEM(events.shape, BF16),
+            pltpu.VMEM((1, tok_rows), jnp.int32),
+            pltpu.VMEM(in_proj.shape, BF16),
+            pltpu.VMEM(filters.shape, F32),
+            pltpu.VMEM((features, tok_rows), F32),
+            pltpu.VMEM((3 * features, tok_rows), BF16),
+            pltpu.SemaphoreType.DMA((4,)),
+        ],
+        10**8, pltpu.HBM, events, positions.reshape(1, tok_rows), in_proj, filters,
+        grant=65500000,
+    )
+    filter_parts = exchange(prepared[:count])
+    got = exchange(prepared[count:])
     own, scale = call(
-        functools.partial(spectrum_kernel, count), "spectrum",
+        functools.partial(spectrum_kernel, count),
         [shape((features, 2 * tok_rows), F32), shape((3 * width, 128), F32)],
-        [pltpu.VMEM((count, width, tok_rows), F32)], 4 * 10**8,
-        high, low, twists, short_filter, skip_gain, *filter_parts,
+        [pltpu.VMEM((count, width, tok_rows), F32)], 4 * 10**8, pltpu.VMEM,
+        high, low, twists, short_filter, skip_gain, length.reshape(1, 1), *filter_parts,
     )
     pairs = [(d, d ^ 1) for d in range(lax.axis_size("batch"))]
     other = lax.ppermute(own, "batch", pairs)
     gated = call(
-        functools.partial(mix_kernel, count), "mix",
+        functools.partial(mix_kernel, count),
         [shape((width, tok_rows), BF16)] * count,
-        [pltpu.VMEM((count, width, tok_rows), BF16)], 2 * 10**9,
+        [pltpu.VMEM((count, width, tok_rows), BF16)], 2 * 10**9, pltpu.VMEM,
         high, low, twists, scale, own, other, *got,
     )
     back = exchange(gated)
     return call(
-        functools.partial(output_kernel, count), "output",
-        shape((tok_rows, features), BF16), [], 10**8, out_proj, *back,
+        functools.partial(output_kernel, count),
+        shape((tok_rows, features), BF16), [], 10**8, pltpu.VMEM, out_proj, *back,
     )
 
 

time: 43.2 us -> 43 us (level)
  Pallas kernels: 5.59 us -> 7.82 us
  local copies, waits for them, and re-layouts: 3.8 us -> 2.05 us
    pallas_call x5 -> x4, Pallas kernels: 5.59 us -> 7.82 us  [call(): pl.pallas_call(kernel, out_shape=out_shape, in_specs=[pl.BlockSpec(memory...]
    unnamed x22 -> x24, local copies, waits for them, and re-layouts: 3.8 us -> 2.05 us
    ppermute x9, waiting for transfers between devices: 17.4 us -> 17 us  [exchange(): lax.ppermute(parts[k], 'seq', [(d, d ^ k) for d in range(count)])]
  transfers between devices with their start and end apart: 10 -> 10, of which waited for: 6 -> 6; matrix products, arithmetic and copies ran while one was open for 0% -> 0% of each run, Pallas kernels for 1% -> 0%
where the time goes in v1:
time: 43 us; the launch traced here: 42.7 us
  waiting for transfers between devices  17 us (40%)
  starting transfers between devices  15.1 us (35%)
  Pallas kernels  7.82 us (18%)
  local copies, waits for them, and re-layouts  2.05 us (5%)
  between operations  0.76 us (2%)
    ppermute x9, waiting for transfers between devices, exchange(): lax.ppermute(parts[k], 'seq', [(d, d ^ k) for d in range(count)])  17 us
    ppermute x9, starting transfers between devices, exchange(): lax.ppermute(parts[k], 'seq', [(d, d ^ k) for d in range(count)])  15 us
    pallas_call x4, Pallas kernels, call(): pl.pallas_call(kernel, out_shape=out_shape, in_specs=[pl.BlockSpec(memory...  7.82 us
    unnamed x24, local copies, waits for them, and re-layouts  2.05 us
  transfers between devices with their start and end apart: 10, of which 6 were waited for; matrix products, arithmetic and copies ran while one was open for 0% of the time, Pallas kernels for 0%

profile of v1, /device:TPU:0, one launch (start us, length us, event | category | flops | bytes accessed | tf_op | source)
XLA Modules:
  0.0 42.7 jit_solution(15377087080349698978)
XLA Ops:
  0.0 2.6 %shard_map.109 = (f32[64,256]{1,0:T(8,128)}, f32[64,256]{1,0:T(8,128)}, f32[64,256]{1,0:T(8,128)}, f32[64,256]{1,0:T(8,128)}, bf16[208,256]{1,0:T(8,128)(2,1)}, ...) custom-call(bf16[256,256]{1,0:T(8,128)(2,1)} %events_hbm.1, s32[1,256]{1,0:T(1,128)} %bitcast.3, ...), custom_call_target="tpu_custom_call" | custom-call | flops 100000000 | bytes 1737728 | tf_op jit(solution)/shard_map/pallas_call | solution.py:253
  2.6 0.0 copy-start.8
  2.7 3.1 %collective-permute-start = (f32[64,256]{1,0:T(8,128)}, f32[64,256]{1,0:T(8,128)S(1)}, u32[]{:S(2)}, u32[]{:S(2)}) collective-permute-start(f32[64,256]{1,0:T(8,128)} %get-tuple-element.20), channel_id=1, source_target_pairs={{0,1},{1,0},{2,3},{3,2},{4,5},{5,4},{6,7},{7,6},{8,9},{9,8},{10,11... | collective-permute-start | bytes 196616 | tf_op jit(solution)/shard_map/ppermute | solution.py:268
  5.8 2.6 %collective-permute-start.1 = (f32[64,256]{1,0:T(8,128)}, f32[64,256]{1,0:T(8,128)S(1)}, u32[]{:S(2)}, u32[]{:S(2)}) collective-permute-start(f32[64,256]{1,0:T(8,128)} %get-tuple-element.21), channel_id=1, source_target_pairs={{0,2},{1,3},{2,0},{3,1},{4,6},{5,7},{6,4},{7,5},{8,10},{9,11},{10,... | collective-permute-start | bytes 196616 | tf_op jit(solution)/shard_map/ppermute | solution.py:268
  8.4 0.0 collective-permute-start.2
  9.0 0.0 copy-start.4
  9.0 0.0 collective-permute-done.refs_1_
  9.1 4.2 %collective-permute-done.1.refs_2_ = f32[64,256]{1,0:T(8,128)S(1)} collective-permute-done((f32[64,256]{1,0:T(8,128)}, f32[64,256]{1,0:T(8,128)S(1)}, u32[]{:S(2)}, u32[]{:S(2)}) %collective-permute-start.1) | collective-permute-done | bytes 65568 | tf_op jit(solution)/shard_map/ppermute | solution.py:268
  13.3 1.4 %collective-permute-done.2.refs_3_ = f32[64,256]{1,0:T(8,128)S(1)} collective-permute-done((f32[64,256]{1,0:T(8,128)}, f32[64,256]{1,0:T(8,128)S(1)}, u32[]{:S(2)}, u32[]{:S(2)}) %collective-permute-start.2) | collective-permute-done | bytes 65568 | tf_op jit(solution)/shard_map/ppermute | solution.py:268
  14.7 0.8 %copy-done.2 = f32[64,256]{1,0:T(8,128)S(1)} copy-done((f32[64,256]{1,0:T(8,128)S(1)}, f32[64,256]{1,0:T(8,128)}, u32[]{:S(2)}) %copy-start.2) | copy-done | bytes 65560
  15.5 1.0 %copy-done.6 = bf16[512,512]{1,0:T(8,128)(2,1)S(1)} copy-done((bf16[512,512]{1,0:T(8,128)(2,1)S(1)}, bf16[512,512]{1,0:T(8,128)(2,1)}, u32[]{:S(2)}) %copy-start.6) | copy-done | bytes 524312
  16.6 0.0 copy-start.7
  16.6 0.7 %shard_map.110 = (f32[256,512]{1,0:T(8,128)S(1)}, f32[192,128]{1,0:T(8,128)S(1)}) custom-call(bf16[512,512]{1,0:T(8,128)(2,1)S(1)} %copy-done.6, bf16[512,512]{1,0:T(8,128)(2,1)S(1)} %copy-done.5, f32[8,256]{1,0:T(8,128)S(1)} %copy-done.8, f32[3,768]{1,0:T(4,128)S(1)} %copy-done.3, f32[2,256]{1,0:T(2,128)S(1)} %copy-done.4, s32[1,1]{1,0:T(1,128)} %bitcast.2.length_ref, ...), custom_call_target="tpu_custom_call" | custom-call | flops 400000000 | bytes 1952772 | tf_op jit(solution)/shard_map/pallas_call | solution.py:253
  17.3 0.1 collective-permute-start.3
  17.4 0.1 copy-done.11
  17.5 0.0 collective-permute-start.4
  17.5 0.0 copy-done.10
  17.5 2.3 %collective-permute-start.5 = (bf16[208,256]{1,0:T(8,128)(2,1)S(1)}, bf16[208,256]{1,0:T(8,128)(2,1)S(1)}, u32[]{:S(2)}, u32[]{:S(2)}) collective-permute-start(bf16[208,256]{1,0:T(8,128)(2,1)S(1)} %copy-done.10), channel_id=1, source_target_pairs={{0,2},{1,3},{2,0},{3,1},{4,6},{5,7},{6,4},{7,5},{8,10},{9,11},{10,... | collective-permute-start | bytes 319496 | tf_op jit(solution)/shard_map/ppermute | solution.py:268
  19.8 2.1 %collective-permute-start.6 = (bf16[208,256]{1,0:T(8,128)(2,1)S(1)}, bf16[208,256]{1,0:T(8,128)(2,1)S(1)}, u32[]{:S(2)}, u32[]{:S(2)}) collective-permute-start(bf16[208,256]{1,0:T(8,128)(2,1)S(1)} %copy-done.9), channel_id=1, source_target_pairs={{0,3},{1,2},{2,1},{3,0},{4,7},{5,6},{6,5},{7,4},{8,11},{9,10},{10,... | collective-permute-start | bytes 319496 | tf_op jit(solution)/shard_map/ppermute | solution.py:268
  21.9 2.9 %collective-permute-done.4.refs_1_ = bf16[208,256]{1,0:T(8,128)(2,1)S(1)} collective-permute-done((bf16[208,256]{1,0:T(8,128)(2,1)S(1)}, bf16[208,256]{1,0:T(8,128)(2,1)S(1)}, u32[]{:S(2)}, u32[]{:S(2)}) %collective-permute-start.4) | collective-permute-done | bytes 106528 | tf_op jit(solution)/shard_map/ppermute | solution.py:268
  24.8 4.1 %collective-permute-done.5.refs_2_ = bf16[208,256]{1,0:T(8,128)(2,1)S(1)} collective-permute-done((bf16[208,256]{1,0:T(8,128)(2,1)S(1)}, bf16[208,256]{1,0:T(8,128)(2,1)S(1)}, u32[]{:S(2)}, u32[]{:S(2)}) %collective-permute-start.5) | collective-permute-done | bytes 106528 | tf_op jit(solution)/shard_map/ppermute | solution.py:268
  28.9 0.0 collective-permute-done.6.refs_3_
  28.9 0.0 collective-permute-done.3.other_ref
  28.9 0.0 copy-start
  28.9 3.5 %shard_map.111 = (bf16[64,256]{1,0:T(8,128)(2,1)S(1)}, bf16[64,256]{1,0:T(8,128)(2,1)S(1)}, bf16[64,256]{1,0:T(8,128)(2,1)S(1)}, bf16[64,256]{1,0:T(8,128)(2,1)S(1)}) custom-call(bf16[512,512]{1,0:T(8,128)(2,1)S(1)} %copy-done.7, bf16[512,512]{1,0:T(8,128)(2,1)S(1)} %copy-done.5, f32[8,256]{1,0:T(8,128)S(1)} %copy-done.8, ...), custom_call_target="tpu_custom_call" | custom-call | flops 2000000000 | bytes 2760704 | tf_op jit(solution)/shard_map/pallas_call | solution.py:253
  32.4 2.3 %collective-permute-start.7 = (bf16[64,256]{1,0:T(8,128)(2,1)S(1)}, bf16[64,256]{1,0:T(8,128)(2,1)S(1)}, u32[]{:S(2)}, u32[]{:S(2)}) collective-permute-start(bf16[64,256]{1,0:T(8,128)(2,1)S(1)} %get-tuple-element.30), channel_id=1, source_target_pairs={{0,1},{1,0},{2,3},{3,2},{4,5},{5,4},{6,7},{7,6},{8,9},{9,8},{10,11... | collective-permute-start | bytes 98312 | tf_op jit(solution)/shard_map/ppermute | solution.py:268
  34.8 1.2 %collective-permute-start.8 = (bf16[64,256]{1,0:T(8,128)(2,1)S(1)}, bf16[64,256]{1,0:T(8,128)(2,1)S(1)}, u32[]{:S(2)}, u32[]{:S(2)}) collective-permute-start(bf16[64,256]{1,0:T(8,128)(2,1)S(1)} %get-tuple-element.31), channel_id=1, source_target_pairs={{0,2},{1,3},{2,0},{3,1},{4,6},{5,7},{6,4},{7,5},{8,10},{9,11},{10,... | collective-permute-start | bytes 98312 | tf_op jit(solution)/shard_map/ppermute | solution.py:268
  36.0 1.4 %collective-permute-start.9 = (bf16[64,256]{1,0:T(8,128)(2,1)S(1)}, bf16[64,256]{1,0:T(8,128)(2,1)S(1)}, u32[]{:S(2)}, u32[]{:S(2)}) collective-permute-start(bf16[64,256]{1,0:T(8,128)(2,1)S(1)} %get-tuple-element.32), channel_id=1, source_target_pairs={{0,3},{1,2},{2,1},{3,0},{4,7},{5,6},{6,5},{7,4},{8,11},{9,10},{10,... | collective-permute-start | bytes 98312 | tf_op jit(solution)/shard_map/ppermute | solution.py:268
  37.4 0.0 collective-permute-done.7.refs_1_
  37.4 2.9 %collective-permute-done.8.refs_2_ = bf16[64,256]{1,0:T(8,128)(2,1)S(1)} collective-permute-done((bf16[64,256]{1,0:T(8,128)(2,1)S(1)}, bf16[64,256]{1,0:T(8,128)(2,1)S(1)}, u32[]{:S(2)}, u32[]{:S(2)}) %collective-permute-start.8) | collective-permute-done | bytes 32800 | tf_op jit(solution)/shard_map/ppermute | solution.py:268
  40.3 1.4 %collective-permute-done.9.refs_3_ = bf16[64,256]{1,0:T(8,128)(2,1)S(1)} collective-permute-done((bf16[64,256]{1,0:T(8,128)(2,1)S(1)}, bf16[64,256]{1,0:T(8,128)(2,1)S(1)}, u32[]{:S(2)}, u32[]{:S(2)}) %collective-permute-start.9) | collective-permute-done | bytes 32800 | tf_op jit(solution)/shard_map/ppermute | solution.py:268
  41.7 1.0 %shard_map.112 = bf16[256,256]{1,0:T(8,128)(2,1)} custom-call(bf16[256,256]{1,0:T(8,128)(2,1)S(1)} %copy-done, bf16[64,256]{1,0:T(8,128)(2,1)S(1)} %get-tuple-element.29.refs_0_, bf16[64,256]{1,0:T(8,128)(2,1)S(1)} %collective-permute-done.7.refs_1_, bf16[64,256]{1,0:T(8,128)(2,1)S(1)} %collective-permute-done.8.refs_2_, ...), custom_call_target="tpu_custom_call" | custom-call | flops 100000000 | bytes 393216 | tf_op jit(solution)/shard_map/pallas_call | solution.py:253
  (16 shorter events, 0.0 us)
Async XLA Ops:
  0.0 14.7 %copy-start.3 = (f32[3,768]{1,0:T(4,128)S(1)}, f32[3,768]{1,0:T(4,128)}, u32[]{:S(2)}) copy-start(f32[3,768]{1,0:T(4,128)} %short_ref.1) | copy-start | bytes 27652
  0.0 14.7 %copy-start.5 = (bf16[512,512]{1,0:T(8,128)(2,1)S(1)}, bf16[512,512]{1,0:T(8,128)(2,1)}, u32[]{:S(2)}) copy-start(bf16[512,512]{1,0:T(8,128)(2,1)} %constant.7.clone.low_ref) | copy-start | bytes 1572868
  2.6 12.0 %copy-start.8 = (f32[8,256]{1,0:T(8,128)S(1)}, f32[8,256]{1,0:T(8,128)}, u32[]{:S(2)}) copy-start(f32[8,256]{1,0:T(8,128)} %constant.8.clone.twist_ref) | copy-start | bytes 24580
  2.7 6.4 %collective-permute-start = (f32[64,256]{1,0:T(8,128)}, f32[64,256]{1,0:T(8,128)S(1)}, u32[]{:S(2)}, u32[]{:S(2)}) collective-permute-start(f32[64,256]{1,0:T(8,128)} %get-tuple-element.20), channel_id=1, source_target_pairs={{0,1},{1,0},{2,3},{3,2},{4,5},{5,4},{6,7},{7,6},{8,9},{9,8},{10,11... | collective-permute-start | bytes 196616 | tf_op jit(solution)/shard_map/ppermute | solution.py:268
  5.8 7.5 %collective-permute-start.1 = (f32[64,256]{1,0:T(8,128)}, f32[64,256]{1,0:T(8,128)S(1)}, u32[]{:S(2)}, u32[]{:S(2)}) collective-permute-start(f32[64,256]{1,0:T(8,128)} %get-tuple-element.21), channel_id=1, source_target_pairs={{0,2},{1,3},{2,0},{3,1},{4,6},{5,7},{6,4},{7,5},{8,10},{9,11},{10,... | collective-permute-start | bytes 196616 | tf_op jit(solution)/shard_map/ppermute | solution.py:268
  8.4 6.3 %collective-permute-start.2 = (f32[64,256]{1,0:T(8,128)}, f32[64,256]{1,0:T(8,128)S(1)}, u32[]{:S(2)}, u32[]{:S(2)}) collective-permute-start(f32[64,256]{1,0:T(8,128)} %get-tuple-element.22), channel_id=1, source_target_pairs={{0,3},{1,2},{2,1},{3,0},{4,7},{5,6},{6,5},{7,4},{8,11},{9,10},{10,... | collective-permute-start | bytes 196616 | tf_op jit(solution)/shard_map/ppermute | solution.py:268
  9.0 5.7 %copy-start.4 = (f32[2,256]{1,0:T(2,128)S(1)}, f32[2,256]{1,0:T(2,128)}, u32[]{:S(2)}) copy-start(f32[2,256]{1,0:T(2,128)} %gain_ref.1) | copy-start | bytes 6148
  14.7 0.8 %copy-start.2 = (f32[64,256]{1,0:T(8,128)S(1)}, f32[64,256]{1,0:T(8,128)}, u32[]{:S(2)}) copy-start(f32[64,256]{1,0:T(8,128)} %get-tuple-element.19.refs_0_) | copy-start | bytes 196612
  15.5 1.0 %copy-start.6 = (bf16[512,512]{1,0:T(8,128)(2,1)S(1)}, bf16[512,512]{1,0:T(8,128)(2,1)}, u32[]{:S(2)}) copy-start(bf16[512,512]{1,0:T(8,128)(2,1)} %constant.6.clone.high_ref) | copy-start | bytes 1572868
  16.6 0.9 %copy-start.11 = (bf16[208,256]{1,0:T(8,128)(2,1)S(1)}, bf16[208,256]{1,0:T(8,128)(2,1)}, u32[]{:S(2)}) copy-start(bf16[208,256]{1,0:T(8,128)(2,1)} %get-tuple-element.26) | copy-start | bytes 319492
  16.6 0.9 %copy-start.10 = (bf16[208,256]{1,0:T(8,128)(2,1)S(1)}, bf16[208,256]{1,0:T(8,128)(2,1)}, u32[]{:S(2)}) copy-start(bf16[208,256]{1,0:T(8,128)(2,1)} %get-tuple-element.27) | copy-start | bytes 319492
  16.6 3.2 %copy-start.9 = (bf16[208,256]{1,0:T(8,128)(2,1)S(1)}, bf16[208,256]{1,0:T(8,128)(2,1)}, u32[]{:S(2)}) copy-start(bf16[208,256]{1,0:T(8,128)(2,1)} %get-tuple-element.28) | copy-start | bytes 319492
  16.6 12.3 %copy-start.1 = (bf16[208,256]{1,0:T(8,128)(2,1)S(1)}, bf16[208,256]{1,0:T(8,128)(2,1)}, u32[]{:S(2)}) copy-start(bf16[208,256]{1,0:T(8,128)(2,1)} %get-tuple-element.25.refs_0_) | copy-start | bytes 319492
  16.6 12.3 %copy-start.7 = (bf16[512,512]{1,0:T(8,128)(2,1)S(1)}, bf16[512,512]{1,0:T(8,128)(2,1)}, u32[]{:S(2)}) copy-start(bf16[512,512]{1,0:T(8,128)(2,1)} %constant.6.clone.high_ref) | copy-start | bytes 1572868
  17.3 11.6 %collective-permute-start.3 = (f32[256,512]{1,0:T(8,128)S(1)}, f32[256,512]{1,0:T(8,128)S(1)}, u32[]{:S(2)}, u32[]{:S(2)}) collective-permute-start(f32[256,512]{1,0:T(8,128)S(1)} %get-tuple-element.24.own_ref), channel_id=1, source_target_pairs={{0,4},{4,0},{8,12},{12,8},{16,20},{20,16},{24,28},{28,24},{1,5},{5... | collective-permute-start | bytes 1572872 | tf_op jit(solution)/shard_map/ppermute | solution.py:304
  17.5 7.3 %collective-permute-start.4 = (bf16[208,256]{1,0:T(8,128)(2,1)S(1)}, bf16[208,256]{1,0:T(8,128)(2,1)S(1)}, u32[]{:S(2)}, u32[]{:S(2)}) collective-permute-start(bf16[208,256]{1,0:T(8,128)(2,1)S(1)} %copy-done.11), channel_id=1, source_target_pairs={{0,1},{1,0},{2,3},{3,2},{4,5},{5,4},{6,7},{7,6},{8,9},{9,8},{10,11... | collective-permute-start | bytes 319496 | tf_op jit(solution)/shard_map/ppermute | solution.py:268
  17.5 11.4 %collective-permute-start.5 = (bf16[208,256]{1,0:T(8,128)(2,1)S(1)}, bf16[208,256]{1,0:T(8,128)(2,1)S(1)}, u32[]{:S(2)}, u32[]{:S(2)}) collective-permute-start(bf16[208,256]{1,0:T(8,128)(2,1)S(1)} %copy-done.10), channel_id=1, source_target_pairs={{0,2},{1,3},{2,0},{3,1},{4,6},{5,7},{6,4},{7,5},{8,10},{9,11},{10,... | collective-permute-start | bytes 319496 | tf_op jit(solution)/shard_map/ppermute | solution.py:268
  19.8 9.1 %collective-permute-start.6 = (bf16[208,256]{1,0:T(8,128)(2,1)S(1)}, bf16[208,256]{1,0:T(8,128)(2,1)S(1)}, u32[]{:S(2)}, u32[]{:S(2)}) collective-permute-start(bf16[208,256]{1,0:T(8,128)(2,1)S(1)} %copy-done.9), channel_id=1, source_target_pairs={{0,3},{1,2},{2,1},{3,0},{4,7},{5,6},{6,5},{7,4},{8,11},{9,10},{10,... | collective-permute-start | bytes 319496 | tf_op jit(solution)/shard_map/ppermute | solution.py:268
  28.9 12.8 %copy-start = (bf16[256,256]{1,0:T(8,128)(2,1)S(1)}, bf16[256,256]{1,0:T(8,128)(2,1)}, u32[]{:S(2)}) copy-start(bf16[256,256]{1,0:T(8,128)(2,1)} %weights_ref.1) | copy-start | bytes 393220
  32.4 5.0 %collective-permute-start.7 = (bf16[64,256]{1,0:T(8,128)(2,1)S(1)}, bf16[64,256]{1,0:T(8,128)(2,1)S(1)}, u32[]{:S(2)}, u32[]{:S(2)}) collective-permute-start(bf16[64,256]{1,0:T(8,128)(2,1)S(1)} %get-tuple-element.30), channel_id=1, source_target_pairs={{0,1},{1,0},{2,3},{3,2},{4,5},{5,4},{6,7},{7,6},{8,9},{9,8},{10,11... | collective-permute-start | bytes 98312 | tf_op jit(solution)/shard_map/ppermute | solution.py:268
  34.8 5.6 %collective-permute-start.8 = (bf16[64,256]{1,0:T(8,128)(2,1)S(1)}, bf16[64,256]{1,0:T(8,128)(2,1)S(1)}, u32[]{:S(2)}, u32[]{:S(2)}) collective-permute-start(bf16[64,256]{1,0:T(8,128)(2,1)S(1)} %get-tuple-element.31), channel_id=1, source_target_pairs={{0,2},{1,3},{2,0},{3,1},{4,6},{5,7},{6,4},{7,5},{8,10},{9,11},{10,... | collective-permute-start | bytes 98312 | tf_op jit(solution)/shard_map/ppermute | solution.py:268
  36.0 5.7 %collective-permute-start.9 = (bf16[64,256]{1,0:T(8,128)(2,1)S(1)}, bf16[64,256]{1,0:T(8,128)(2,1)S(1)}, u32[]{:S(2)}, u32[]{:S(2)}) collective-permute-start(bf16[64,256]{1,0:T(8,128)(2,1)S(1)} %get-tuple-element.32), channel_id=1, source_target_pairs={{0,3},{1,2},{2,1},{3,0},{4,7},{5,6},{6,5},{7,4},{8,11},{9,10},{10,... | collective-permute-start | bytes 98312 | tf_op jit(solution)/shard_map/ppermute | solution.py:268

commit v2 on v1

--- a/solution.py
+++ b/solution.py
@@ -11,7 +11,7 @@
 
 F32 = jnp.float32
 BF16 = jnp.bfloat16
-META = 16
+META = 8
 NT = (((1,), (1,)), ((), ()))
 NN = (((1,), (0,)), ((), ()))
 TN = (((0,), (0,)), ((), ()))
@@ -101,37 +101,29 @@
     return blocks
 
 
-def prepare_kernel(count, events_hbm, pos_hbm, weights_hbm, filt_hbm, *refs):
-    taps, rows_out = refs[:count], refs[count : 2 * count]
-    events_ref, pos_ref, weights_ref, filt_ref, flipped, whole, sems = refs[2 * count :]
+def filter_kernel(count, filt_ref, *refs):
+    taps, flipped = refs[:count], refs[count]
     me = lax.axis_index("seq")
     core = lax.rem(lax.axis_index("batch"), 2)
-    loads = [
-        pltpu.make_async_copy(source, target, sems.at[n])
-        for n, (source, target) in enumerate((
-            (events_hbm, events_ref),
-            (weights_hbm, weights_ref),
-            (filt_hbm, filt_ref),
-            (pos_hbm, pos_ref),
-        ))
-    ]
-    for load in loads:
-        load.start()
+    half = lax.rem(lax.div(lax.axis_index("batch"), 2), 2)
+    share = taps[0].shape[0]
+    one = jnp.where(core == 0, filt_ref[:, 0, :], filt_ref[:, 1, :])
+    flipped[...] = one.T
+    for k in range(count):
+        start = pl.multiple_of((2 * lax.bitwise_xor(me, k) + half) * share, share)
+        taps[k][...] = flipped[pl.ds(start, share), :]
+
+
+def project_kernel(count, events_ref, weights_ref, pos_ref, *refs):
+    rows_out, whole = refs[:count], refs[count]
+    me = lax.axis_index("seq")
     rows, features = events_ref.shape
     width = features // count
-    loads[2].wait()
-    one = jnp.where(core == 0, filt_ref[:, 0, :], filt_ref[:, 1, :])
-    flipped[...] = one.T
-    for k in range(count):
-        start = pl.multiple_of(lax.bitwise_xor(me, k) * width, width)
-        taps[k][...] = flipped[pl.ds(start, width), :]
-    for n in (0, 1, 3):
-        loads[n].wait()
-    pos = pos_ref[...]
     projected = lax.dot_general(
         weights_ref[...], events_ref[...], (((0,), (1,)), ((), ())), preferred_element_type=F32
     )
     whole[...] = projected.astype(BF16)
+    pos = pos_ref[...]
     line = lax.broadcasted_iota(jnp.int32, (META, rows), 0)
     high = lax.div(pos, 256)
     meta = jnp.where(line == 0, high, jnp.where(line == 1, pos - high * 256, 0))
@@ -144,13 +136,28 @@
         rows_out[k][3 * width :, :] = meta
 
 
+def gather_kernel(count, *refs):
+    parts, out_ref = refs[:count], refs[count]
+    me = lax.axis_index("seq")
+    share = parts[0].shape[0]
+    for k in range(count):
+        start = pl.multiple_of(lax.bitwise_xor(me, k) * share, share)
+        out_ref[pl.ds(start, share), :] = parts[k][...]
+
+
 def spectrum_kernel(count, high_ref, low_ref, twist_ref, short_ref, gain_ref, length_ref, *refs):
-    parts, spec_ref, scale_ref, held = refs[:count], refs[count], refs[count + 1], refs[count + 2]
-    me = lax.axis_index("seq")
-    width, inner = parts[0].shape
-    for k in range(count):
-        held[pl.ds(lax.bitwise_xor(me, k), 1)] = parts[k][...][None]
-    real, imag = forward([held[n] for n in range(count)], high_ref, low_ref, twist_ref)
+    own_ref, other_ref, spec_ref, scale_ref = refs
+    me = lax.axis_index("seq")
+    half = lax.rem(lax.div(lax.axis_index("batch"), 2), 2)
+    share, inner = own_ref.shape[0] // count, own_ref.shape[1]
+    width = 2 * share
+    own, other = own_ref[...], other_ref[...]
+    lower, upper = jnp.where(half == 0, own, other), jnp.where(half == 0, other, own)
+    blocks = [
+        jnp.concatenate([part[n * share : (n + 1) * share] for part in (lower, upper)], axis=0)
+        for n in range(count)
+    ]
+    real, imag = forward(blocks, high_ref, low_ref, twist_ref)
     spec_ref[:, :inner] = real
     spec_ref[:, inner:] = imag
     features = gain_ref.shape[1]
@@ -261,11 +268,15 @@
     )(*args)
 
 
+def hops(count):
+    return [*range(count // 2, count), *range(1, count // 2)]
+
+
 def exchange(parts):
     count = len(parts)
-    got = [parts[0]]
-    for k in range(1, count):
-        got.append(lax.ppermute(parts[k], "seq", [(d, d ^ k) for d in range(count)]))
+    got = [parts[0]] * count
+    for k in hops(count):
+        got[k] = lax.ppermute(parts[k], "seq", [(d, d ^ k) for d in range(count)])
     return got
 
 
@@ -276,31 +287,32 @@
     shape = jax.ShapeDtypeStruct
     high, low, twists = (jnp.asarray(t) for t in tables(count, tok_rows))
 
-    prepared = call(
-        functools.partial(prepare_kernel, count),
-        [shape((width, tok_rows), F32)] * count
-        + [shape((3 * width + META, tok_rows), BF16)] * count,
-        [
-            pltpu.VMEM(events.shape, BF16),
-            pltpu.VMEM((1, tok_rows), jnp.int32),
-            pltpu.VMEM(in_proj.shape, BF16),
-            pltpu.VMEM(filters.shape, F32),
-            pltpu.VMEM((features, tok_rows), F32),
-            pltpu.VMEM((3 * features, tok_rows), BF16),
-            pltpu.SemaphoreType.DMA((4,)),
-        ],
-        10**8, pltpu.HBM, events, positions.reshape(1, tok_rows), in_proj, filters,
-        grant=65500000,
-    )
-    filter_parts = exchange(prepared[:count])
-    got = exchange(prepared[count:])
+    taps = call(
+        functools.partial(filter_kernel, count),
+        [shape((width // 2, tok_rows), F32)] * count,
+        [pltpu.VMEM((features, tok_rows), F32)], 10**6, pltpu.VMEM, filters,
+    )
+    rows = call(
+        functools.partial(project_kernel, count),
+        [shape((3 * width + META, tok_rows), BF16)] * count,
+        [pltpu.VMEM((3 * features, tok_rows), BF16)], 10**8, pltpu.VMEM,
+        events, in_proj, positions.reshape(1, tok_rows),
+    )
+    filter_parts = exchange(taps)
+    got = exchange(rows)
+    groups = lax.axis_size("batch")
+    half = call(
+        functools.partial(gather_kernel, count),
+        shape((features // 2, tok_rows), F32), [], 10**6, pltpu.VMEM, *filter_parts,
+    )
+    other_half = lax.ppermute(half, "batch", [(d, d ^ 2) for d in range(groups)])
     own, scale = call(
         functools.partial(spectrum_kernel, count),
         [shape((features, 2 * tok_rows), F32), shape((3 * width, 128), F32)],
-        [pltpu.VMEM((count, width, tok_rows), F32)], 4 * 10**8, pltpu.VMEM,
-        high, low, twists, short_filter, skip_gain, length.reshape(1, 1), *filter_parts,
-    )
-    pairs = [(d, d ^ 1) for d in range(lax.axis_size("batch"))]
+        [], 4 * 10**8, pltpu.VMEM,
+        high, low, twists, short_filter, skip_gain, length.reshape(1, 1), half, other_half,
+    )
+    pairs = [(d, d ^ 1) for d in range(groups)]
     other = lax.ppermute(own, "batch", pairs)
     gated = call(
         functools.partial(mix_kernel, count),

time: 43 us -> 44.3 us (1.030)
  Pallas kernels: 7.82 us -> 5.79 us
  waiting for transfers between devices: 17 us -> 18.6 us
  starting transfers between devices: 15.1 us -> 16.2 us
  local copies, waits for them, and re-layouts: 2.05 us -> 2.74 us
    pallas_call x4 -> x6, Pallas kernels: 7.82 us -> 5.79 us  [call(): pl.pallas_call(kernel, out_shape=out_shape, in_specs=[pl.BlockSpec(memory...]
    ppermute x9 -> x10, waiting for transfers between devices: 17 us -> 18.6 us  [the longest x9 15.7 us: exchange(): got[k] = lax.ppermute(parts[k], 'seq', [(d, d ^ k) for d in range(count)])]
    ppermute x9 -> x10, starting transfers between devices: 15 us -> 16.2 us  [the longest x9 14.6 us: exchange(): got[k] = lax.ppermute(parts[k], 'seq', [(d, d ^ k) for d in range(count)])]
    unnamed x24 -> x22, local copies, waits for them, and re-layouts: 2.05 us -> 2.74 us
  transfers between devices with their start and end apart: 10 -> 11, of which waited for: 6 -> 7; matrix products, arithmetic and copies ran while one was open for 0% -> 0% of each run, Pallas kernels for 0% -> 1%
where the time goes in v2:
time: 44.3 us; the launch traced here: 44.1 us
  waiting for transfers between devices  18.6 us (42%)
  starting transfers between devices  16.2 us (37%)
  Pallas kernels  5.79 us (13%)
  local copies, waits for them, and re-layouts  2.74 us (6%)
  between operations  0.77 us (2%)
    ppermute x9, waiting for transfers between devices, exchange(): got[k] = lax.ppermute(parts[k], 'seq', [(d, d ^ k) for d in range(count)])  15.7 us
    ppermute x9, starting transfers between devices, exchange(): got[k] = lax.ppermute(parts[k], 'seq', [(d, d ^ k) for d in range(count)])  14.6 us
    pallas_call x6, Pallas kernels, call(): pl.pallas_call(kernel, out_shape=out_shape, in_specs=[pl.BlockSpec(memory...  5.79 us
    ppermute x1, waiting for transfers between devices, body(): lax.ppermute(half, 'batch', [(d, d ^ 2) for d in range(groups)])  2.83 us
    unnamed x22, local copies, waits for them, and re-layouts  2.74 us
    ppermute x1, starting transfers between devices, body(): lax.ppermute(half, 'batch', [(d, d ^ 2) for d in range(groups)])  1.56 us
  transfers between devices with their start and end apart: 11, of which 7 were waited for; matrix products, arithmetic and copies ran while one was open for 0% of the time, Pallas kernels for 1%

profile of v2, /device:TPU:0, one launch (start us, length us, event | category | flops | bytes accessed | tf_op | source)
XLA Modules:
  0.0 44.1 jit_solution(3734164770656280739)
XLA Ops:
  0.0 1.0 %copy-done = f32[256,2,256]{2,1,0:T(2,128)S(1)} copy-done((f32[256,2,256]{2,1,0:T(2,128)S(1)}, f32[256,2,256]{2,1,0:T(2,128)}, u32[]{:S(2)}) %copy-start) | copy-done | bytes 524312
  1.0 0.2 shard_map.109
  1.3 3.1 %collective-permute-start = (f32[32,256]{1,0:T(8,128)S(1)}, f32[32,256]{1,0:T(8,128)S(1)}, u32[]{:S(2)}, u32[]{:S(2)}) collective-permute-start(f32[32,256]{1,0:T(8,128)S(1)} %get-tuple-element.20), channel_id=1, source_target_pairs={{0,1},{1,0},{2,3},{3,2},{4,5},{5,4},{6,7},{7,6},{8,9},{9,8},{10,11... | collective-permute-start | bytes 98312 | tf_op jit(solution)/shard_map/ppermute | solution.py:279
  4.4 2.6 %collective-permute-start.1 = (f32[32,256]{1,0:T(8,128)S(1)}, f32[32,256]{1,0:T(8,128)S(1)}, u32[]{:S(2)}, u32[]{:S(2)}) collective-permute-start(f32[32,256]{1,0:T(8,128)S(1)} %get-tuple-element.21), channel_id=1, source_target_pairs={{0,2},{1,3},{2,0},{3,1},{4,6},{5,7},{6,4},{7,5},{8,10},{9,11},{10,... | collective-permute-start | bytes 98312 | tf_op jit(solution)/shard_map/ppermute | solution.py:279
  7.0 2.8 %collective-permute-done.1.refs_2_ = f32[32,256]{1,0:T(8,128)S(1)} collective-permute-done((f32[32,256]{1,0:T(8,128)S(1)}, f32[32,256]{1,0:T(8,128)S(1)}, u32[]{:S(2)}, u32[]{:S(2)}) %collective-permute-start.1) | collective-permute-done | bytes 32800 | tf_op jit(solution)/shard_map/ppermute | solution.py:279
  9.8 2.9 %collective-permute-done.2.refs_3_ = f32[32,256]{1,0:T(8,128)S(1)} collective-permute-done((f32[32,256]{1,0:T(8,128)S(1)}, f32[32,256]{1,0:T(8,128)S(1)}, u32[]{:S(2)}, u32[]{:S(2)}) %collective-permute-start.2) | collective-permute-done | bytes 32800 | tf_op jit(solution)/shard_map/ppermute | solution.py:279
  12.7 0.0 copy-start.6
  12.7 1.6 %collective-permute-start.3 = (f32[128,256]{1,0:T(8,128)S(1)}, f32[128,256]{1,0:T(8,128)S(1)}, u32[]{:S(2)}, u32[]{:S(2)}) collective-permute-start(f32[128,256]{1,0:T(8,128)S(1)} %shard_map.110.refs_0_), channel_id=1, source_target_pairs={{0,8},{4,12},{8,0},{12,4},{16,24},{20,28},{24,16},{28,20},{1,9},{5... | collective-permute-start | bytes 393224 | tf_op jit(solution)/shard_map/ppermute | solution.py:308
  14.9 2.8 %collective-permute-done.3.refs_1_ = f32[128,256]{1,0:T(8,128)S(1)} collective-permute-done((f32[128,256]{1,0:T(8,128)S(1)}, f32[128,256]{1,0:T(8,128)S(1)}, u32[]{:S(2)}, u32[]{:S(2)}) %collective-permute-start.3) | collective-permute-done | bytes 131104 | tf_op jit(solution)/shard_map/ppermute | solution.py:308
  17.8 0.0 copy-start.8
  17.8 1.0 %copy-done.8 = bf16[512,512]{1,0:T(8,128)(2,1)S(1)} copy-done((bf16[512,512]{1,0:T(8,128)(2,1)S(1)}, bf16[512,512]{1,0:T(8,128)(2,1)}, u32[]{:S(2)}) %copy-start.8) | copy-done | bytes 524312
  18.8 0.7 %shard_map.111 = (f32[256,512]{1,0:T(8,128)S(1)}, f32[192,128]{1,0:T(8,128)S(1)}) custom-call(bf16[512,512]{1,0:T(8,128)(2,1)S(1)} %copy-done.8, bf16[512,512]{1,0:T(8,128)(2,1)S(1)} %copy-done.7, f32[8,256]{1,0:T(8,128)S(1)} %copy-done.10, f32[3,768]{1,0:T(4,128)S(1)} %copy-done.5, f32[2,256]{1,0:T(2,128)S(1)} %copy-done.6, s32[1,1]{1,0:T(1,128)} %bitcast.2.length_ref, ...), custom_call_target="tpu_custom_call" | custom-call | flops 400000000 | bytes 1952772 | tf_op jit(solution)/shard_map/pallas_call | solution.py:260
  19.5 0.0 copy-start.4
  19.5 0.0 copy-start.9
  19.6 0.1 collective-permute-start.4
  19.6 0.2 copy-done.1
  19.8 0.0 copy-done.3
  19.9 0.4 copy-done.4
  20.3 0.3 shard_map.112
  20.6 0.1 collective-permute-start.5
  20.7 0.9 %collective-permute-start.6 = (bf16[200,256]{1,0:T(8,128)(2,1)S(1)}, bf16[200,256]{1,0:T(8,128)(2,1)S(1)}, u32[]{:S(2)}, u32[]{:S(2)}) collective-permute-start(bf16[200,256]{1,0:T(8,128)(2,1)S(1)} %get-tuple-element.27), channel_id=1, source_target_pairs={{0,2},{1,3},{2,0},{3,1},{4,6},{5,7},{6,4},{7,5},{8,10},{9,11},{10,... | collective-permute-start | bytes 307208 | tf_op jit(solution)/shard_map/ppermute | solution.py:279
  21.6 3.5 %collective-permute-start.7 = (bf16[200,256]{1,0:T(8,128)(2,1)S(1)}, bf16[200,256]{1,0:T(8,128)(2,1)S(1)}, u32[]{:S(2)}, u32[]{:S(2)}) collective-permute-start(bf16[200,256]{1,0:T(8,128)(2,1)S(1)} %get-tuple-element.28), channel_id=1, source_target_pairs={{0,3},{1,2},{2,1},{3,0},{4,7},{5,6},{6,5},{7,4},{8,11},{9,10},{10,... | collective-permute-start | bytes 307208 | tf_op jit(solution)/shard_map/ppermute | solution.py:279
  25.1 1.5 %collective-permute-done.5.refs_1_ = bf16[200,256]{1,0:T(8,128)(2,1)S(1)} collective-permute-done((bf16[200,256]{1,0:T(8,128)(2,1)S(1)}, bf16[200,256]{1,0:T(8,128)(2,1)S(1)}, u32[]{:S(2)}, u32[]{:S(2)}) %collective-permute-start.5) | collective-permute-done | bytes 102432 | tf_op jit(solution)/shard_map/ppermute | solution.py:279
  26.5 5.3 %collective-permute-done.6.refs_2_ = bf16[200,256]{1,0:T(8,128)(2,1)S(1)} collective-permute-done((bf16[200,256]{1,0:T(8,128)(2,1)S(1)}, bf16[200,256]{1,0:T(8,128)(2,1)S(1)}, u32[]{:S(2)}, u32[]{:S(2)}) %collective-permute-start.6) | collective-permute-done | bytes 102432 | tf_op jit(solution)/shard_map/ppermute | solution.py:279
  31.8 0.0 copy-start.2
  31.8 3.5 %shard_map.113 = (bf16[64,256]{1,0:T(8,128)(2,1)S(1)}, bf16[64,256]{1,0:T(8,128)(2,1)S(1)}, bf16[64,256]{1,0:T(8,128)(2,1)S(1)}, bf16[64,256]{1,0:T(8,128)(2,1)S(1)}) custom-call(bf16[512,512]{1,0:T(8,128)(2,1)S(1)} %copy-done.9, bf16[512,512]{1,0:T(8,128)(2,1)S(1)} %copy-done.7, f32[8,256]{1,0:T(8,128)S(1)} %copy-done.10, ...), custom_call_target="tpu_custom_call" | custom-call | flops 2000000000 | bytes 2744320 | tf_op jit(solution)/shard_map/pallas_call | solution.py:260
  35.4 1.8 %collective-permute-start.8 = (bf16[64,256]{1,0:T(8,128)(2,1)S(1)}, bf16[64,256]{1,0:T(8,128)(2,1)S(1)}, u32[]{:S(2)}, u32[]{:S(2)}) collective-permute-start(bf16[64,256]{1,0:T(8,128)(2,1)S(1)} %get-tuple-element.30), channel_id=1, source_target_pairs={{0,1},{1,0},{2,3},{3,2},{4,5},{5,4},{6,7},{7,6},{8,9},{9,8},{10,11... | collective-permute-start | bytes 98312 | tf_op jit(solution)/shard_map/ppermute | solution.py:279
  37.1 0.3 collective-permute-start.9
  37.4 2.4 %collective-permute-start.10 = (bf16[64,256]{1,0:T(8,128)(2,1)S(1)}, bf16[64,256]{1,0:T(8,128)(2,1)S(1)}, u32[]{:S(2)}, u32[]{:S(2)}) collective-permute-start(bf16[64,256]{1,0:T(8,128)(2,1)S(1)} %get-tuple-element.32), channel_id=1, source_target_pairs={{0,3},{1,2},{2,1},{3,0},{4,7},{5,6},{6,5},{7,4},{8,11},{9,10},{10,... | collective-permute-start | bytes 98312 | tf_op jit(solution)/shard_map/ppermute | solution.py:279
  39.8 2.2 %collective-permute-done.9.refs_2_ = bf16[64,256]{1,0:T(8,128)(2,1)S(1)} collective-permute-done((bf16[64,256]{1,0:T(8,128)(2,1)S(1)}, bf16[64,256]{1,0:T(8,128)(2,1)S(1)}, u32[]{:S(2)}, u32[]{:S(2)}) %collective-permute-start.9) | collective-permute-done | bytes 32800 | tf_op jit(solution)/shard_map/ppermute | solution.py:279
  42.0 1.1 %collective-permute-done.10.refs_3_ = bf16[64,256]{1,0:T(8,128)(2,1)S(1)} collective-permute-done((bf16[64,256]{1,0:T(8,128)(2,1)S(1)}, bf16[64,256]{1,0:T(8,128)(2,1)S(1)}, u32[]{:S(2)}, u32[]{:S(2)}) %collective-permute-start.10) | collective-permute-done | bytes 32800 | tf_op jit(solution)/shard_map/ppermute | solution.py:279
  43.1 1.0 %shard_map.114 = bf16[256,256]{1,0:T(8,128)(2,1)} custom-call(bf16[256,256]{1,0:T(8,128)(2,1)S(1)} %copy-done.2, bf16[64,256]{1,0:T(8,128)(2,1)S(1)} %get-tuple-element.29.refs_0_, bf16[64,256]{1,0:T(8,128)(2,1)S(1)} %collective-permute-done.8.refs_1_, bf16[64,256]{1,0:T(8,128)(2,1)S(1)} %collective-permute-done.9.refs_2_, ...), custom_call_target="tpu_custom_call" | custom-call | flops 100000000 | bytes 393216 | tf_op jit(solution)/shard_map/pallas_call | solution.py:260
  (18 shorter events, 0.1 us)
Async XLA Ops:
  0.0 1.0 %copy-start = (f32[256,2,256]{2,1,0:T(2,128)S(1)}, f32[256,2,256]{2,1,0:T(2,128)}, u32[]{:S(2)}) copy-start(f32[256,2,256]{2,1,0:T(2,128)} %filt_ref.1) | copy-start | bytes 1572868
  1.0 16.7 %copy-start.7 = (bf16[512,512]{1,0:T(8,128)(2,1)S(1)}, bf16[512,512]{1,0:T(8,128)(2,1)}, u32[]{:S(2)}) copy-start(bf16[512,512]{1,0:T(8,128)(2,1)} %constant.7.clone.low_ref) | copy-start | bytes 1572868
  1.3 5.7 %collective-permute-start = (f32[32,256]{1,0:T(8,128)S(1)}, f32[32,256]{1,0:T(8,128)S(1)}, u32[]{:S(2)}, u32[]{:S(2)}) collective-permute-start(f32[32,256]{1,0:T(8,128)S(1)} %get-tuple-element.20), channel_id=1, source_target_pairs={{0,1},{1,0},{2,3},{3,2},{4,5},{5,4},{6,7},{7,6},{8,9},{9,8},{10,11... | collective-permute-start | bytes 98312 | tf_op jit(solution)/shard_map/ppermute | solution.py:279
  4.4 5.4 %collective-permute-start.1 = (f32[32,256]{1,0:T(8,128)S(1)}, f32[32,256]{1,0:T(8,128)S(1)}, u32[]{:S(2)}, u32[]{:S(2)}) collective-permute-start(f32[32,256]{1,0:T(8,128)S(1)} %get-tuple-element.21), channel_id=1, source_target_pairs={{0,2},{1,3},{2,0},{3,1},{4,6},{5,7},{6,4},{7,5},{8,10},{9,11},{10,... | collective-permute-start | bytes 98312 | tf_op jit(solution)/shard_map/ppermute | solution.py:279
  7.0 5.7 %collective-permute-start.2 = (f32[32,256]{1,0:T(8,128)S(1)}, f32[32,256]{1,0:T(8,128)S(1)}, u32[]{:S(2)}, u32[]{:S(2)}) collective-permute-start(f32[32,256]{1,0:T(8,128)S(1)} %get-tuple-element.22), channel_id=1, source_target_pairs={{0,3},{1,2},{2,1},{3,0},{4,7},{5,6},{6,5},{7,4},{8,11},{9,10},{10,... | collective-permute-start | bytes 98312 | tf_op jit(solution)/shard_map/ppermute | solution.py:279
  12.7 5.1 %copy-start.5 = (f32[3,768]{1,0:T(4,128)S(1)}, f32[3,768]{1,0:T(4,128)}, u32[]{:S(2)}) copy-start(f32[3,768]{1,0:T(4,128)} %short_ref.1) | copy-start | bytes 27652
  12.7 5.1 %copy-start.10 = (f32[8,256]{1,0:T(8,128)S(1)}, f32[8,256]{1,0:T(8,128)}, u32[]{:S(2)}) copy-start(f32[8,256]{1,0:T(8,128)} %constant.8.clone.twist_ref) | copy-start | bytes 24580
  12.7 5.1 %copy-start.6 = (f32[2,256]{1,0:T(2,128)S(1)}, f32[2,256]{1,0:T(2,128)}, u32[]{:S(2)}) copy-start(f32[2,256]{1,0:T(2,128)} %gain_ref.1) | copy-start | bytes 6148
  12.7 5.0 %collective-permute-start.3 = (f32[128,256]{1,0:T(8,128)S(1)}, f32[128,256]{1,0:T(8,128)S(1)}, u32[]{:S(2)}, u32[]{:S(2)}) collective-permute-start(f32[128,256]{1,0:T(8,128)S(1)} %shard_map.110.refs_0_), channel_id=1, source_target_pairs={{0,8},{4,12},{8,0},{12,4},{16,24},{20,28},{24,16},{28,20},{1,9},{5... | collective-permute-start | bytes 393224 | tf_op jit(solution)/shard_map/ppermute | solution.py:308
  17.8 1.0 %copy-start.8 = (bf16[512,512]{1,0:T(8,128)(2,1)S(1)}, bf16[512,512]{1,0:T(8,128)(2,1)}, u32[]{:S(2)}) copy-start(bf16[512,512]{1,0:T(8,128)(2,1)} %constant.6.clone.high_ref) | copy-start | bytes 1572868
  18.8 1.0 %copy-start.1 = (bf16[256,768]{1,0:T(8,128)(2,1)S(1)}, bf16[256,768]{1,0:T(8,128)(2,1)}, u32[]{:S(2)}) copy-start(bf16[256,768]{1,0:T(8,128)(2,1)} %weights_ref.2) | copy-start | bytes 1179652
  18.8 1.0 %copy-start.3 = (bf16[256,256]{1,0:T(8,128)(2,1)S(1)}, bf16[256,256]{1,0:T(8,128)(2,1)}, u32[]{:S(2)}) copy-start(bf16[256,256]{1,0:T(8,128)(2,1)} %events_ref.1) | copy-start | bytes 393220
  19.5 0.7 %copy-start.4 = (s32[256]{0:T(256)S(1)}, s32[256]{0:T(256)}, u32[]{:S(2)}) copy-start(s32[256]{0:T(256)} %param.12) | copy-start | bytes 3076
  19.5 12.3 %copy-start.9 = (bf16[512,512]{1,0:T(8,128)(2,1)S(1)}, bf16[512,512]{1,0:T(8,128)(2,1)}, u32[]{:S(2)}) copy-start(bf16[512,512]{1,0:T(8,128)(2,1)} %constant.6.clone.high_ref) | copy-start | bytes 1572868
  19.6 12.2 %collective-permute-start.4 = (f32[256,512]{1,0:T(8,128)S(1)}, f32[256,512]{1,0:T(8,128)S(1)}, u32[]{:S(2)}, u32[]{:S(2)}) collective-permute-start(f32[256,512]{1,0:T(8,128)S(1)} %get-tuple-element.24.own_ref), channel_id=1, source_target_pairs={{0,4},{4,0},{8,12},{12,8},{16,20},{20,16},{24,28},{28,24},{1,5},{5... | collective-permute-start | bytes 1572872 | tf_op jit(solution)/shard_map/ppermute | solution.py:316
  20.6 5.9 %collective-permute-start.5 = (bf16[200,256]{1,0:T(8,128)(2,1)S(1)}, bf16[200,256]{1,0:T(8,128)(2,1)S(1)}, u32[]{:S(2)}, u32[]{:S(2)}) collective-permute-start(bf16[200,256]{1,0:T(8,128)(2,1)S(1)} %get-tuple-element.26), channel_id=1, source_target_pairs={{0,1},{1,0},{2,3},{3,2},{4,5},{5,4},{6,7},{7,6},{8,9},{9,8},{10,11... | collective-permute-start | bytes 307208 | tf_op jit(solution)/shard_map/ppermute | solution.py:279
  20.7 11.1 %collective-permute-start.6 = (bf16[200,256]{1,0:T(8,128)(2,1)S(1)}, bf16[200,256]{1,0:T(8,128)(2,1)S(1)}, u32[]{:S(2)}, u32[]{:S(2)}) collective-permute-start(bf16[200,256]{1,0:T(8,128)(2,1)S(1)} %get-tuple-element.27), channel_id=1, source_target_pairs={{0,2},{1,3},{2,0},{3,1},{4,6},{5,7},{6,4},{7,5},{8,10},{9,11},{10,... | collective-permute-start | bytes 307208 | tf_op jit(solution)/shard_map/ppermute | solution.py:279
  21.6 10.2 %collective-permute-start.7 = (bf16[200,256]{1,0:T(8,128)(2,1)S(1)}, bf16[200,256]{1,0:T(8,128)(2,1)S(1)}, u32[]{:S(2)}, u32[]{:S(2)}) collective-permute-start(bf16[200,256]{1,0:T(8,128)(2,1)S(1)} %get-tuple-element.28), channel_id=1, source_target_pairs={{0,3},{1,2},{2,1},{3,0},{4,7},{5,6},{6,5},{7,4},{8,11},{9,10},{10,... | collective-permute-start | bytes 307208 | tf_op jit(solution)/shard_map/ppermute | solution.py:279
  31.8 11.3 %copy-start.2 = (bf16[256,256]{1,0:T(8,128)(2,1)S(1)}, bf16[256,256]{1,0:T(8,128)(2,1)}, u32[]{:S(2)}) copy-start(bf16[256,256]{1,0:T(8,128)(2,1)} %weights_ref.3) | copy-start | bytes 393220
  35.4 4.5 %collective-permute-start.8 = (bf16[64,256]{1,0:T(8,128)(2,1)S(1)}, bf16[64,256]{1,0:T(8,128)(2,1)S(1)}, u32[]{:S(2)}, u32[]{:S(2)}) collective-permute-start(bf16[64,256]{1,0:T(8,128)(2,1)S(1)} %get-tuple-element.30), channel_id=1, source_target_pairs={{0,1},{1,0},{2,3},{3,2},{4,5},{5,4},{6,7},{7,6},{8,9},{9,8},{10,11... | collective-permute-start | bytes 98312 | tf_op jit(solution)/shard_map/ppermute | solution.py:279
  37.1 4.9 %collective-permute-start.9 = (bf16[64,256]{1,0:T(8,128)(2,1)S(1)}, bf16[64,256]{1,0:T(8,128)(2,1)S(1)}, u32[]{:S(2)}, u32[]{:S(2)}) collective-permute-start(bf16[64,256]{1,0:T(8,128)(2,1)S(1)} %get-tuple-element.31), channel_id=1, source_target_pairs={{0,2},{1,3},{2,0},{3,1},{4,6},{5,7},{6,4},{7,5},{8,10},{9,11},{10,... | collective-permute-start | bytes 98312 | tf_op jit(solution)/shard_map/ppermute | solution.py:279
  37.4 5.7 %collective-permute-start.10 = (bf16[64,256]{1,0:T(8,128)(2,1)S(1)}, bf16[64,256]{1,0:T(8,128)(2,1)S(1)}, u32[]{:S(2)}, u32[]{:S(2)}) collective-permute-start(bf16[64,256]{1,0:T(8,128)(2,1)S(1)} %get-tuple-element.32), channel_id=1, source_target_pairs={{0,3},{1,2},{2,1},{3,0},{4,7},{5,6},{6,5},{7,4},{8,11},{9,10},{10,... | collective-permute-start | bytes 98312 | tf_op jit(solution)/shard_map/ppermute | solution.py:279
